TPU v7x, 512 devices: a whole 4x8x8 slice. The times are simulated.
512 devices in a mesh: team: 16 (over y, core), cuts: 32 (over z, x).
Axes of the slice: x: 4, y: 8, z: 8, core: 2. Of those that a mesh axis runs over, the one named last changes fastest.
Arguments:
- position: float32 [3, 131072], P(None, ('team', 'cuts')), may hold values from -6 to 6
- velocity: float32 [3, 131072], P(None, ('team', 'cuts')), may hold values from -3 to 3
- accel_old: float32 [3, 131072], P(None, ('team', 'cuts')), may hold values from -6 to 6
- jerk_old: float32 [3, 131072], P(None, ('team', 'cuts')), may hold values from -16 to 16
- star_mass: float32 [131072], P(('team', 'cuts')), may hold values from 0.2 to 5
- active_index: int32 [16384], P(('team', 'cuts')), may hold values from 0 to 255, as said below
- active_count: int32 [512], P(('team', 'cuts')), may hold values from 1 to 32, 8192 in all
Outputs:
- corrected: float32 [12, 16384], P(None, ('team', 'cuts'))
Inputs may be any that keep to these rules, and one draw needn't show every extreme that they name: `active_index`: each device's 32 entries are distinct. `active_count`: the counts of all devices sum to 8192.
All inputs are finite; a program needn't handle non-finite values.
Results may differ from a plain program's by a relative error of at most 0.00025.
Values sent between devices are 32-bit elements; how exact they have to be, the bound alone decides.
A program may use at most 64 MiB of HBM per device.

v0:
```python
import math

import jax
import jax.numpy as jnp
from jax import lax
from jax.sharding import PartitionSpec as P

STEP_DT = 0.5
SOFTENING = 0.0004


def predict(position, velocity, accel_old, jerk_old):
    pred_pos = position + STEP_DT * (
        velocity + STEP_DT * (accel_old * 0.5 + STEP_DT * (jerk_old * (1.0 / 6.0)))
    )
    pred_vel = velocity + STEP_DT * (accel_old + STEP_DT * (jerk_old * 0.5))
    return (pred_pos, pred_vel)


def pair_sums(sinks, field_pos, field_vel, weights):
    separation = [
        field_pos[component][:, None] - sinks[component][None, :] for component in range(3)
    ]
    relative = [
        field_vel[component][:, None] - sinks[3 + component][None, :] for component in range(3)
    ]
    radius_sq = (
        separation[0] * separation[0]
        + separation[1] * separation[1]
        + separation[2] * separation[2]
        + SOFTENING
    )
    inverse = lax.rsqrt(radius_sq)
    strength = weights[:, None] * (inverse * inverse * inverse)
    radial = (
        3.0
        * (separation[0] * relative[0] + separation[1] * relative[1] + separation[2] * relative[2])
        * (inverse * inverse)
    )
    rows = [jnp.sum(strength * separation[component], axis=0) for component in range(3)]
    rows = rows + [
        jnp.sum(strength * (relative[component] - radial * separation[component]), axis=0)
        for component in range(3)
    ]
    return jnp.stack(rows)


def pair_field(sinks, field_pos, field_vel, weights):
    width = sinks.shape[1]
    field_rows = field_pos.shape[1]
    block_size = math.gcd(width, max(8, 262144 // field_rows))
    block_total = width // block_size

    def one_block(block_index, result):
        sink_block = lax.dynamic_slice_in_dim(sinks, block_index * block_size, block_size, 1)
        sums = pair_sums(sink_block, field_pos, field_vel, weights)
        return lax.dynamic_update_slice_in_dim(result, sums, block_index * block_size, 1)

    return lax.fori_loop(0, block_total, one_block, jnp.zeros((6, width), jnp.float32))


def correct(sink_state, old_acc, old_jerk, new_rows, is_live):
    pred_pos = sink_state[:3]
    pred_vel = sink_state[3:]
    new_acc = new_rows[:3]
    new_jerk = new_rows[3:]
    change = old_acc - new_acc
    second = -6.0 * change - STEP_DT * (4.0 * old_jerk + 2.0 * new_jerk)
    third = 12.0 * change + 6.0 * STEP_DT * (old_jerk + new_jerk)
    new_pos = pred_pos + STEP_DT * STEP_DT * (second * (1.0 / 24.0) + third * (1.0 / 120.0))
    new_vel = pred_vel + STEP_DT * (second * (1.0 / 6.0) + third * (1.0 / 24.0))
    stacked = jnp.concatenate([new_pos, new_vel, new_acc, new_jerk], axis=0)
    return jnp.where(is_live[None, :], stacked, 0.0)


def gather_states(states):
    within_team = lax.all_gather(states, "team", axis=1, tiled=True)
    return lax.all_gather(within_team, "cuts", axis=1, tiled=True)


def reduce_partials(partials):
    per_group = lax.psum_scatter(partials, "cuts", scatter_dimension=1, tiled=True)
    return lax.psum_scatter(per_group, "team", scatter_dimension=1, tiled=True)


def local(position, velocity, accel_old, jerk_old, star_mass, active_index, active_count):
    pred_pos, pred_vel = predict(position, velocity, accel_old, jerk_old)
    own_state = jnp.concatenate(
        [jnp.take(pred_pos, active_index, axis=1), jnp.take(pred_vel, active_index, axis=1)], axis=0
    )
    slot_count = active_index.shape[0]
    stars_total = position.shape[1] * lax.axis_size("team") * lax.axis_size("cuts")
    weights = star_mass / stars_total
    gathered = gather_states(own_state)
    partials = pair_field(gathered, pred_pos, pred_vel, weights)
    new_rows = reduce_partials(partials)
    is_live = jnp.arange(slot_count, dtype=jnp.int32) < active_count[0]
    old_acc = jnp.take(accel_old, active_index, axis=1)
    old_jerk = jnp.take(jerk_old, active_index, axis=1)
    return correct(own_state, old_acc, old_jerk, new_rows, is_live)


def solution(mesh):
    in_specs = (
        P(None, ("team", "cuts")),
        P(None, ("team", "cuts")),
        P(None, ("team", "cuts")),
        P(None, ("team", "cuts")),
        P(("team", "cuts")),
        P(("team", "cuts")),
        P(("team", "cuts")),
    )
    out_specs = P(None, ("team", "cuts"))
    return jax.shard_map(local, mesh=mesh, in_specs=in_specs, out_specs=out_specs, check_vma=False)
```

profile of v0, /device:TPU:1, one launch (start us, length us, event | category | flops | bytes accessed | tf_op | source)
XLA Modules:
  0.0 418.5 jit_solution(14460809103251882108)
XLA Ops:
  6.5 0.7 compare_select_fusion
  7.2 0.7 compare_and_fusion
  7.9 0.7 multiply_add_fusion
  8.6 0.1 copy.102
  8.8 0.6 gather_fusion.2
  9.4 0.1 copy.103
  9.4 0.1 copy.98
  9.6 0.6 gather_fusion
  10.2 0.1 copy.99
  10.3 21.0 %all-gather = f32[16,32,6]{1,2,0:T(8,128)S(1)} all-gather(f32[1,32,6]{1,2,0:T(8,128)S(1)} %maximum_bitcast_fusion), channel_id=1, replica_groups=mesh['team'=16,'cuts'=32] {'team'}, dimensions={0}, use_global_device_ids=true | all-gather | bytes 13056 | tf_op jit(solution)/shard_map/all_gather | solution.py:77
  31.3 0.1 reshape.53
  31.4 42.2 %all_gather.7 = f32[6,16384]{1,0:T(8,128)S(1)} all-gather(f32[6,512]{1,0:T(8,128)S(1)} %bitcast.105), channel_id=1, replica_groups=mesh['team'=16,'cuts'=32] {'cuts'}, dimensions={1}, use_global_device_ids=true | all-gather | bytes 405504 | tf_op jit(solution)/shard_map/all_gather | solution.py:78
  73.6 50.1 %while.13 = (s32[]{:T(128)}, f32[6,16384]{1,0:T(8,128)S(1)}, f32[256]{0:T(256)S(1)}, f32[3,256]{1,0:T(4,128)S(1)}, f32[6,16384]{1,0:T(8,128)S(1)}, /*index=5*/f3...) while((s32[]{:T(128)}, f32[6,16384]{1,0:T(8,128)S(1)}, ...), condition=%wide.region_7.0_spmd, body=%wide.region_0.8_spmd.sunk | while | flops 10479627 | bytes 232723 | solution.py:59
  73.6 0.1 fusion.30
  73.7 2.9 fusion.32
  76.6 0.1 stack.50
  76.7 0.1 fusion.30
  76.9 2.9 fusion.32
  79.8 0.1 stack.50
  79.9 0.1 fusion.30
  80.0 2.9 fusion.32
  82.9 0.1 stack.50
  83.0 0.1 fusion.30
  83.1 2.9 fusion.32
  86.0 0.1 stack.50
  86.1 0.1 fusion.30
  86.3 2.9 fusion.32
  89.3 0.1 fusion.30
  89.4 2.9 fusion.32
  92.3 0.1 stack.50
  92.4 0.1 fusion.30
  92.5 2.9 fusion.32
  95.4 0.1 stack.50
  95.5 0.1 fusion.30
  95.7 2.9 fusion.32
  98.6 0.1 stack.50
  98.7 0.1 fusion.30
  98.8 2.9 fusion.32
  101.8 0.1 fusion.30
  101.9 2.9 fusion.32
  104.9 0.1 fusion.30
  105.1 2.9 fusion.32
  108.1 0.1 fusion.30
  108.2 2.9 fusion.32
  111.2 0.1 fusion.30
  111.3 2.9 fusion.32
  114.3 0.1 fusion.30
  114.5 2.9 fusion.32
  117.5 0.1 fusion.30
  117.6 2.9 fusion.32
  120.6 0.1 fusion.30
  120.8 2.9 fusion.32
  123.7 0.8 copy-done
  125.2 221.2 %reduce-scatter.5.cloned.1.call-done = f32[6,512]{1,0:T(8,128)} async-done(((f32[6,16384]{1,0:T(8,128)}), f32[6,512]{1,0:T(8,128)}) %reduce-scatter.5.cloned.1.call-update) | async-done | bytes 12304 | tf_op jit(solution)/shard_map/reduce_scatter | solution.py:82
  346.4 1.6 copy.107
  348.0 0.1 copy.100
  348.1 0.1 copy.105
  348.3 0.6 gather_fusion.1
  348.9 0.1 copy.101
  348.9 0.6 gather_fusion.3
  349.5 0.1 copy.106
  349.6 60.6 %reduce-scatter.7.cloned.1.call-done = f32[32,6]{1,0:T(8,128)} async-done(((f32[512,6]{1,0:T(8,128)}), f32[32,6]{1,0:T(8,128)}) %reduce-scatter.7.cloned.1.call-update) | async-done | bytes 784
  410.2 0.8 copy.108
  411.0 0.6 maximum_select_fusion
  (61 shorter events, 0.9 us)
Async XLA Ops:
  6.5 1.4 copy-start.1
  6.5 1.4 copy-start.2
  6.5 339.9 %reduce-scatter.5.cloned.1.call-start = ((), (), s32[]{:S(2)}) async-start(), calls=%async_computation.2 | async-start | bytes 540672 | tf_op jit(solution)/shard_map/reduce_scatter | solution.py:82
  31.4 42.2 %copy-start.3 = (f32[256]{0:T(256)S(1)}, f32[256]{0:T(256)}, u32[]{:S(2)}) copy-start(f32[256]{0:T(256)} %param.15) | copy-start | bytes 3076
  123.7 0.8 copy-start
  124.5 285.7 %reduce-scatter.7.cloned.1.call-start = ((), (), s32[]{:S(2)}) async-start(), calls=%async_computation.3 | async-start | bytes 278528
Sparse Core Ops, SparseCore 0:
  124.7 221.6 reduce-scatter.4
  349.2 61.0 reduce-scatter.6
where the time goes:
time: 420 us; the launch traced here: 418 us
  waiting for transfers between devices  282 us (67%)
  blocking collectives  63.2 us (15%)
  other arithmetic  49 us (12%)
  between operations  14.2 us (3%)
  local copies, waits for them, and re-layouts  9.52 us (2%)
    reduce_scatter x1, waiting for transfers between devices, reduce_partials(): lax.psum_scatter(partials, 'cuts', scatter_dimension=1, tiled=True)  221 us
    unnamed x3, waiting for transfers between devices  60.7 us
    reduce_sum x16, other arithmetic, pair_sums(): jnp.sum(strength * (relative[component] - radial * separation[component])...  46.2 us
    all_gather x1, blocking collectives, gather_states(): return lax.all_gather(within_team, 'cuts', axis=1, tiled=True)  42.2 us
    all_gather x1, blocking collectives, gather_states(): within_team = lax.all_gather(states, 'team', axis=1, tiled=True)  21 us
  transfers between devices with their start and end apart: 2, of which 2 were waited for; matrix products, arithmetic and copies ran while one was open for 0% of the time, Pallas kernels for 0%

commit v1 on v0

v1 whole, which is shorter than its diff:
```python
import functools

import jax
import jax.numpy as jnp
from jax import lax
from jax.experimental import pallas as pl
from jax.experimental.pallas import tpu as pltpu
from jax.sharding import PartitionSpec as P

STEP_DT = 0.5
SOFTENING = 0.0004
MESH = pl.DeviceIdType.MESH
F32 = jnp.float32
BF16 = jnp.bfloat16
NT = (((1,), (1,)), ((), ()))


def split2(value):
    high = value.astype(BF16)
    return high, (value - high.astype(F32)).astype(BF16)


def split3(value):
    high = value.astype(BF16)
    rest = value - high.astype(F32)
    middle = rest.astype(BF16)
    return high, middle, (rest - middle.astype(F32)).astype(BF16)


def stack_pieces(rows, height):
    filled = sum(row.shape[0] for row in rows)
    rows = [row.astype(F32) for row in rows]
    rows = rows + [jnp.zeros((height - filled, rows[0].shape[1]), F32)]
    return jnp.concatenate(rows, axis=0).astype(BF16)


def predict(position, velocity, accel_old, jerk_old):
    pred_pos = position + STEP_DT * (
        velocity + STEP_DT * (accel_old * 0.5 + STEP_DT * (jerk_old * (1.0 / 6.0)))
    )
    pred_vel = velocity + STEP_DT * (accel_old + STEP_DT * (jerk_old * 0.5))
    return (pred_pos, pred_vel)


def correct(sink_state, old_acc, old_jerk, new_rows, is_live):
    pred_pos = sink_state[:3]
    pred_vel = sink_state[3:6]
    new_acc = new_rows[:3]
    new_jerk = new_rows[3:6]
    change = old_acc - new_acc
    second = -6.0 * change - STEP_DT * (4.0 * old_jerk + 2.0 * new_jerk)
    third = 12.0 * change + 6.0 * STEP_DT * (old_jerk + new_jerk)
    new_pos = pred_pos + STEP_DT * STEP_DT * (second * (1.0 / 24.0) + third * (1.0 / 120.0))
    new_vel = pred_vel + STEP_DT * (second * (1.0 / 6.0) + third * (1.0 / 24.0))
    stacked = jnp.concatenate([new_pos, new_vel, new_acc, new_jerk], axis=0)
    return jnp.where(is_live, stacked, 0.0)


def step_kernel(
    teams, cuts, xs, slots, stars,
    pos_ref, vel_ref, acc_ref, jerk_ref, mass_ref, index_ref, count_ref, out_ref,
    own_ref, star_ref, sink_ref, part_ref, sum_ref, weight_ref, wide_ref, lhs_ref, total_ref,
    star_send, star_recv, sink_send, sink_recv, part_send, part_recv,
):
    team = lax.axis_index("team")
    cut = lax.axis_index("cuts")
    zs = cuts // xs
    my_z = cut // xs
    my_x = lax.rem(cut, xs)
    chunk_devices = 2 * xs
    chunk = chunk_devices * slots
    tile = 16

    barrier = pltpu.get_barrier_semaphore()

    def greet_team(k, _):
        pl.semaphore_signal(
            barrier, inc=1, device_id=(lax.rem(team + k, teams), cut), device_id_type=MESH
        )
        return 0

    def greet_cuts(k, _):
        pl.semaphore_signal(
            barrier, inc=1, device_id=(team, lax.rem(cut + k, cuts)), device_id_type=MESH
        )
        return 0

    lax.fori_loop(1, teams, greet_team, 0)
    lax.fori_loop(1, cuts, greet_cuts, 0)

    acc_old = acc_ref[...]
    jerk_old = jerk_ref[...]
    pred_pos, pred_vel = predict(pos_ref[...], vel_ref[...], acc_old, jerk_old)
    weight = mass_ref[...] * (1.0 / (stars * teams * cuts))
    star_ref[team] = jnp.concatenate(
        [pred_pos, pred_vel, weight, jnp.zeros((1, stars), F32)], axis=0
    )
    picked = (
        lax.broadcasted_iota(jnp.int32, (stars, slots), 0) == index_ref[...]
    ).astype(F32).astype(BF16)
    source = jnp.concatenate([pred_pos, pred_vel, acc_old, jerk_old, jnp.zeros((4, stars), F32)], 0)
    pieces = split3(source)
    own = jnp.zeros((16, slots), F32)
    for piece in pieces:
        own = own + jnp.dot(piece, picked, preferred_element_type=F32)
    own_ref[...] = own
    sink_ref[cut] = jnp.concatenate([own[0:8], jnp.zeros((8, 128 - slots), F32)], axis=1)

    pl.semaphore_wait(barrier, teams + cuts - 2)

    def sink_copy(slot, device):
        return pltpu.make_async_remote_copy(
            src_ref=sink_ref.at[slot], dst_ref=sink_ref.at[slot],
            send_sem=sink_send.at[device], recv_sem=sink_recv.at[slot],
            device_id=(team, device), device_id_type=MESH,
        )

    def star_copy(slot, device):
        return pltpu.make_async_remote_copy(
            src_ref=star_ref.at[slot], dst_ref=star_ref.at[slot],
            send_sem=star_send.at[device], recv_sem=star_recv.at[slot],
            device_id=(device, cut), device_id_type=MESH,
        )

    def part_copy(source, slot, device):
        return pltpu.make_async_remote_copy(
            src_ref=part_ref.at[source], dst_ref=sum_ref.at[slot],
            send_sem=part_send.at[source], recv_sem=part_recv.at[slot],
            device_id=(team, device), device_id_type=MESH,
        )

    def send_star(k, _):
        star_copy(team, lax.rem(team + k, teams)).start()
        return 0

    def send_sink(k, _):
        sink_copy(cut, lax.rem(cut + k, cuts)).start()
        return 0

    lax.fori_loop(1, teams, send_star, 0)
    lax.fori_loop(1, cuts, send_sink, 0)

    def star_weights(block):
        state = star_ref[block]
        mass = state[6:7]
        mass_pos = mass * state[0:3]
        mass_vel = mass * state[3:6]
        empty3 = jnp.zeros((3, stars), F32)
        empty9 = jnp.zeros((9, stars), F32)
        plain = stack_pieces([*split3(mass_pos), *split3(mass_vel), *split3(mass), empty3], 32)
        cross = stack_pieces([empty9, *split3(-3.0 * mass_pos), empty3, *split3(3.0 * mass)], 32)
        weight_ref[block] = jnp.concatenate([plain, plain, cross, cross], axis=1)

    def take_star(k, _):
        block = lax.rem(team + k, teams)
        star_copy(block, block).wait_recv()
        star_weights(block)
        return 0

    star_weights(team)
    lax.fori_loop(1, teams, take_star, 0)

    def take_sink(k, _):
        block = lax.rem(cut + k, cuts)
        sink_copy(block, block).wait_recv()
        return 0

    lax.fori_loop(1, cuts, take_sink, 0)

    def fill(block, buffer):
        state = star_ref[block]
        for step in range(chunk // tile):
            rows = slice(step * tile, (step + 1) * tile)
            sinks = [wide_ref[c, rows, :] for c in range(6)]
            sinks = [jnp.concatenate([value] * (stars // 128), axis=1) for value in sinks]
            sep = [state[c : c + 1] - sinks[c] for c in range(3)]
            rel = [state[3 + c : 4 + c] - sinks[3 + c] for c in range(3)]
            radius_sq = sep[0] * sep[0] + (sep[1] * sep[1] + (sep[2] * sep[2] + SOFTENING))
            radial = sep[0] * rel[0] + sep[1] * rel[1] + sep[2] * rel[2]
            inverse = lax.rsqrt(radius_sq)
            inverse_sq = inverse * inverse
            cube = inverse_sq * inverse
            fifth = (cube * inverse_sq) * radial
            for part, value in enumerate((*split2(cube), *split2(fifth))):
                lhs_ref[buffer, rows, part * stars : (part + 1) * stars] = value

    def add(block, buffer):
        total_ref[...] += lax.dot_general(
            lhs_ref[buffer], weight_ref[block], NT, preferred_element_type=F32
        )

    def one_chunk(g, _):
        devices = []
        for side in range(2):
            z = lax.rem(my_z + (zs // 2 - 1 - g if side == 0 else zs // 2 + g), zs)
            for j in range(xs):
                devices.append(z * xs + lax.rem(my_x + j, xs))
        states = []
        for i, device in enumerate(devices):
            state = sink_ref[device]
            states.append(state[:, :slots])
            columns = jnp.transpose(state)[:slots, :]
            for c in range(6):
                wide_ref[c, i * slots : (i + 1) * slots, :] = jnp.broadcast_to(
                    columns[:, c : c + 1], (slots, 128)
                )
        total_ref[...] = jnp.zeros_like(total_ref)
        fill(0, 0)

        def two_blocks(k, _):
            block = 2 * k
            fill(block + 1, 1)
            add(block, 0)
            fill(jnp.minimum(block + 2, teams - 1), 0)
            add(block + 1, 1)
            return 0

        lax.fori_loop(0, teams // 2, two_blocks, 0)
        sums = jnp.concatenate([total_ref[...], jnp.zeros((chunk, 96), F32)], axis=1)
        for i, device in enumerate(devices):
            rows = jnp.transpose(
                jnp.concatenate([sums[i * slots : (i + 1) * slots], jnp.zeros((128 - slots, 128), F32)], 0)
            )
            state = sink_ref[device]
            pos = state[0:3]
            vel = state[3:6]
            whole = rows[18:19] + rows[19:20] + rows[20:21]
            cross = rows[21:22] + rows[22:23] + rows[23:24]
            new_acc = (rows[0:3] + rows[3:6] + rows[6:9]) - pos * whole
            new_jerk = (rows[9:12] + rows[12:15] + rows[15:18]) - vel * whole + pos * cross
            result = jnp.concatenate([new_acc, new_jerk, jnp.zeros((2, 128), F32)], axis=0)
            if i == 0:
                mine = g == zs // 2 - 1

                @pl.when(mine)
                def _():
                    sum_ref[cut] = result

                @pl.when(jnp.logical_not(mine))
                def _():
                    part_ref[device] = result
                    part_copy(device, cut, device).start()
            else:
                part_ref[device] = result
                part_copy(device, cut, device).start()
        return 0

    lax.fori_loop(0, zs // 2, one_chunk, 0)

    def take_part(k, total):
        block = lax.rem(cut + k, cuts)
        part_copy(block, block, block).wait_recv()
        return total + sum_ref[block]

    total = lax.fori_loop(1, cuts, take_part, sum_ref[cut])
    own_rows = own_ref[...]
    is_live = lax.broadcasted_iota(jnp.int32, (1, slots), 1) < count_ref[...]
    out_ref[...] = correct(
        own_rows[0:6], own_rows[6:9], own_rows[9:12], total[:, :slots], is_live
    )

    def end_star(k, _):
        device = lax.rem(team + k, teams)
        star_copy(team, device).wait_send()
        return 0

    def end_sink(k, _):
        device = lax.rem(cut + k, cuts)
        sink_copy(cut, device).wait_send()
        part_copy(device, cut, device).wait_send()
        return 0

    lax.fori_loop(1, teams, end_star, 0)
    lax.fori_loop(1, cuts, end_sink, 0)


def solution(mesh):
    teams = mesh.shape["team"]
    cuts = mesh.shape["cuts"]
    xs = 4

    def local(position, velocity, accel_old, jerk_old, star_mass, active_index, active_count):
        stars = position.shape[1]
        slots = active_index.shape[0]
        chunk = 2 * xs * slots
        vmem = pl.BlockSpec(memory_space=pltpu.VMEM)
        dma = pltpu.SemaphoreType.DMA
        return pl.pallas_call(
            functools.partial(step_kernel, teams, cuts, xs, slots, stars),
            out_shape=jax.ShapeDtypeStruct((12, slots), F32),
            in_specs=[vmem] * 7,
            out_specs=vmem,
            scratch_shapes=[
                pltpu.VMEM((16, slots), F32),
                pltpu.VMEM((teams, 8, stars), F32),
                pltpu.VMEM((cuts, 8, 128), F32),
                pltpu.VMEM((cuts, 8, 128), F32),
                pltpu.VMEM((cuts, 8, 128), F32),
                pltpu.VMEM((teams, 32, 4 * stars), BF16),
                pltpu.VMEM((6, chunk, 128), F32),
                pltpu.VMEM((2, chunk, 4 * stars), BF16),
                pltpu.VMEM((chunk, 32), F32),
                dma((teams,)), dma((teams,)), dma((cuts,)), dma((cuts,)), dma((cuts,)), dma((cuts,)),
            ],
            compiler_params=pltpu.CompilerParams(collective_id=0, has_side_effects=True),
            name="hermite_step",
        )(
            position, velocity, accel_old, jerk_old,
            star_mass.reshape(1, stars), active_index.reshape(1, slots), active_count.reshape(1, 1),
        )

    column = P(None, ("team", "cuts"))
    line = P(("team", "cuts"))
    return jax.shard_map(
        local, mesh=mesh, in_specs=(column, column, column, column, line, line, line),
        out_specs=column, check_vma=False,
    )
```

time: 420 us -> 57.2 us (0.14)
  waiting for transfers between devices: 282 us -> 0 us
  blocking collectives: 63.2 us -> 0 us
  Pallas kernels: 0 us -> 55.1 us
  other arithmetic: 49 us -> 0 us
  between operations: 14.2 us -> 0.66 us
  local copies, waits for them, and re-layouts: 9.52 us -> 1.3 us
    reduce_scatter x1 -> x0, waiting for transfers between devices: 221 us -> none  [reduce_partials(): lax.psum_scatter(partials, 'cuts', scatter_dimension=1, tiled=True)]
    all_gather x2 -> x0, blocking collectives: 63.2 us -> none  [the longest x1 42.2 us: gather_states(): return lax.all_gather(within_team, 'cuts', axis=1, tiled=True)]
    unnamed x3 -> x0, waiting for transfers between devices: 60.7 us -> none
    pallas_call x0 -> x1, Pallas kernels: none -> 55.1 us  [local(): pl.pallas_call(functools.partial(step_kernel, teams, cuts, xs, slots, sta...]
    reduce_sum x16 -> x0, other arithmetic: 46.2 us -> none  [pair_sums(): jnp.sum(strength * (relative[component] - radial * separation[component])...]
  transfers between devices with their start and end apart: 2 -> 0, of which waited for: 2 -> 0; matrix products, arithmetic and copies ran while one was open for 0% -> 0% of each run, Pallas kernels for 0% -> 0%
where the time goes in v1:
time: 57.2 us; the launch traced here: 57 us
  Pallas kernels  55.1 us (96%)
  local copies, waits for them, and re-layouts  1.3 us (2%)
  between operations  0.66 us (1%)
    pallas_call x1, Pallas kernels, local(): pl.pallas_call(functools.partial(step_kernel, teams, cuts, xs, slots, sta...  55.1 us
    unnamed x1, local copies, waits for them, and re-layouts  1.3 us

profile of v1, /device:TPU:1, one launch (start us, length us, event | category | flops | bytes accessed | tf_op | source)
XLA Modules:
  0.0 57.0 jit_solution(661274635420155146)
XLA Ops:
  0.7 55.1 %hermite_step.1 = f32[12,32]{1,0:T(8,128)} custom-call(f32[3,256]{1,0:T(4,128)} %pos_ref.1, f32[3,256]{1,0:T(4,128)} %vel_ref.1, f32[3,256]{1,0:T(4,128)} %acc_ref.1, f32[3,256]{1,0:T(4,128)} %jerk_ref.1, f32[1,256]{1,0:T(1,128)} %bitcast.4, s32[1,32]{1,0:T(1,128)} %bitcast.5, s32[1,1]{1,0:T(1,128)} %bitcast.3.count_ref), custom_call_target="tpu_custom_call" | custom-call | tf_op jit(solution)/shard_map/hermite_step/pallas_call | solution.py:288
  55.7 1.3 %copy.10 = f32[12,32]{1,0:T(8,128)} copy(f32[12,32]{1,0:T(8,128)} %hermite_step.1) | data formatting | bytes 3072

commit v2 on v1

v2 whole, which is shorter than its diff:
```python
import functools

import jax
import jax.numpy as jnp
from jax import lax
from jax.experimental import pallas as pl
from jax.experimental.pallas import tpu as pltpu
from jax.sharding import PartitionSpec as P

STEP_DT = 0.5
SOFTENING = 0.0004
MESH = pl.DeviceIdType.MESH
F32 = jnp.float32
BF16 = jnp.bfloat16


def split2(value):
    high = value.astype(BF16)
    return high, (value - high.astype(F32)).astype(BF16)


def split3(value):
    high = value.astype(BF16)
    rest = value - high.astype(F32)
    middle = rest.astype(BF16)
    return high, middle, (rest - middle.astype(F32)).astype(BF16)


def stack_pieces(rows, height):
    filled = sum(row.shape[0] for row in rows)
    rows = [row.astype(F32) for row in rows]
    rows = rows + [jnp.zeros((height - filled, rows[0].shape[1]), F32)]
    return jnp.concatenate(rows, axis=0).astype(BF16)


def predict(position, velocity, accel_old, jerk_old):
    pred_pos = position + STEP_DT * (
        velocity + STEP_DT * (accel_old * 0.5 + STEP_DT * (jerk_old * (1.0 / 6.0)))
    )
    pred_vel = velocity + STEP_DT * (accel_old + STEP_DT * (jerk_old * 0.5))
    return (pred_pos, pred_vel)


def correct(sink_state, old_acc, old_jerk, new_rows, is_live):
    pred_pos = sink_state[:3]
    pred_vel = sink_state[3:6]
    new_acc = new_rows[:3]
    new_jerk = new_rows[3:6]
    change = old_acc - new_acc
    second = -6.0 * change - STEP_DT * (4.0 * old_jerk + 2.0 * new_jerk)
    third = 12.0 * change + 6.0 * STEP_DT * (old_jerk + new_jerk)
    new_pos = pred_pos + STEP_DT * STEP_DT * (second * (1.0 / 24.0) + third * (1.0 / 120.0))
    new_vel = pred_vel + STEP_DT * (second * (1.0 / 6.0) + third * (1.0 / 24.0))
    stacked = jnp.concatenate([new_pos, new_vel, new_acc, new_jerk], axis=0)
    return jnp.where(is_live, stacked, 0.0)


def step_kernel(
    teams, cuts, xs, slots, stars, cores,
    pos_ref, vel_ref, acc_ref, jerk_ref, mass_ref, index_ref, count_ref, out_ref,
    own_ref, star_ref, sink_ref, part_ref, sum_ref, plain_ref, cross_ref, wide_ref,
    star_send, star_recv, sink_send, sink_recv, part_send, part_recv,
):
    team = lax.axis_index("team")
    cut = lax.axis_index("cuts")
    zs = cuts // xs
    ys = teams // cores
    my_z = cut // xs
    my_x = lax.rem(cut, xs)
    my_y = team // cores
    my_core = lax.rem(team, cores)
    group = xs * slots
    tile = 16
    tiles = 2 * group // tile

    barrier = pltpu.get_barrier_semaphore()

    def greet_team(k, _):
        pl.semaphore_signal(
            barrier, inc=1, device_id=(lax.rem(team + k, teams), cut), device_id_type=MESH
        )
        return 0

    def greet_cuts(k, _):
        pl.semaphore_signal(
            barrier, inc=1, device_id=(team, lax.rem(cut + k, cuts)), device_id_type=MESH
        )
        return 0

    lax.fori_loop(1, teams, greet_team, 0)
    lax.fori_loop(1, cuts, greet_cuts, 0)

    acc_old = acc_ref[...]
    jerk_old = jerk_ref[...]
    pred_pos, pred_vel = predict(pos_ref[...], vel_ref[...], acc_old, jerk_old)
    weight = mass_ref[...] * (1.0 / (stars * teams * cuts))
    star_ref[team] = jnp.concatenate(
        [pred_pos, pred_vel, weight, jnp.zeros((1, stars), F32)], axis=0
    )
    index = jnp.concatenate(
        [index_ref[...], jnp.full((1, 256 - slots), -1, jnp.int32)], axis=1
    )
    picked = (
        lax.broadcasted_iota(jnp.int32, (stars, 256), 0) == index
    ).astype(F32).astype(BF16)
    source = jnp.concatenate([pred_pos, pred_vel, acc_old, jerk_old, jnp.zeros((4, stars), F32)], 0)

    def pick(pick_acc):
        pltpu.matmul_push_rhs(picked, staging_register=0, mxu_index=0)
        for n, piece in enumerate(split3(source)):
            pltpu.matmul_acc_lhs(pick_acc, piece, load_staged_rhs=0 if n == 0 else None)
        own_ref[...] = pltpu.matmul_pop(pick_acc)[:, :slots]

    pl.run_scoped(pick, pltpu.ACC(0)((16, 256), F32))
    own = own_ref[...]
    lane_x = lax.broadcasted_iota(jnp.int32, (8, group), 1) // slots
    state = jnp.concatenate([own[0:6], jnp.zeros((2, slots), F32)], axis=0)
    sink_ref[cut] = jnp.where(lane_x == my_x, jnp.concatenate([state] * xs, axis=1), 0.0)

    def star_weights(block):
        state = star_ref[block]
        mass = state[6:7]
        mass_pos = mass * state[0:3]
        mass_vel = mass * state[3:6]
        empty3 = jnp.zeros((3, stars), F32)
        empty9 = jnp.zeros((9, stars), F32)
        plain_ref[block, :32, :] = stack_pieces(
            [*split3(mass_pos), *split3(mass_vel), *split3(mass), empty3], 32
        )
        cross_ref[block, :32, :] = stack_pieces(
            [empty9, *split3(-3.0 * mass_pos), empty3, *split3(3.0 * mass)], 32
        )

    plain_ref[...] = jnp.zeros_like(plain_ref)
    cross_ref[...] = jnp.zeros_like(cross_ref)
    star_weights(team)

    pl.semaphore_wait(barrier, teams + cuts - 2)

    def sink_copy(slot, device):
        return pltpu.make_async_remote_copy(
            src_ref=sink_ref.at[slot], dst_ref=sink_ref.at[slot],
            send_sem=sink_send.at[device], recv_sem=sink_recv.at[slot],
            device_id=(team, device), device_id_type=MESH,
        )

    def star_copy(slot, device):
        return pltpu.make_async_remote_copy(
            src_ref=star_ref.at[slot], dst_ref=star_ref.at[slot],
            send_sem=star_send.at[device], recv_sem=star_recv.at[slot],
            device_id=(device, cut), device_id_type=MESH,
        )

    def part_copy(z, slot, device):
        return pltpu.make_async_remote_copy(
            src_ref=part_ref.at[z], dst_ref=sum_ref.at[slot],
            send_sem=part_send.at[device], recv_sem=part_recv.at[slot],
            device_id=(team, device), device_id_type=MESH,
        )

    def nth_block(k):
        step = k // cores
        y = (step + 1) // 2 * (2 * lax.rem(step, 2) - 1)
        y = lax.rem(my_y + y + ys, ys)
        return y * cores + lax.rem(my_core + k, cores)

    def send_star(k, _):
        star_copy(team, nth_block(k)).start()
        return 0

    def send_sink(k, _):
        sink_copy(cut, lax.rem(cut + k, cuts)).start()
        return 0

    lax.fori_loop(1, cuts, send_sink, 0)
    lax.fori_loop(1, teams, send_star, 0)

    def devices_of(offset):
        z = lax.rem(my_z + offset, zs)
        return z, [z * xs + lax.rem(my_x + j, xs) for j in range(xs)]

    def open_chunk(offsets, first):
        states = []
        for side, offset in enumerate(offsets):
            _, devices = devices_of(offset)
            for device in devices[1:] if first and side == 0 else devices:
                sink_copy(device, device).wait_recv()
            state = sink_ref[devices[0]]
            for device in devices[1:]:
                state = state + sink_ref[device]
            columns = jnp.transpose(state)
            for c in range(6):
                wide_ref[c, side * group : (side + 1) * group, :] = jnp.broadcast_to(
                    columns[:, c : c + 1], (group, 128)
                )
            states.append(state)
        return states

    def pairs(block, plain_acc, cross_acc):
        pltpu.matmul_push_rhs(plain_ref[block], staging_register=0, mxu_index=0, transpose=True)
        pltpu.matmul_push_rhs(cross_ref[block], staging_register=0, mxu_index=1, transpose=True)
        state = star_ref[block]
        for step in range(tiles):
            rows = slice(step * tile, (step + 1) * tile)
            sinks = [wide_ref[c, rows, :] for c in range(6)]
            sinks = [jnp.concatenate([value] * (stars // 128), axis=1) for value in sinks]
            sep = [state[c : c + 1] - sinks[c] for c in range(3)]
            rel = [state[3 + c : 4 + c] - sinks[3 + c] for c in range(3)]
            radius_sq = sep[0] * sep[0] + (sep[1] * sep[1] + (sep[2] * sep[2] + SOFTENING))
            radial = sep[0] * rel[0] + sep[1] * rel[1] + sep[2] * rel[2]
            inverse = lax.rsqrt(radius_sq)
            inverse_sq = inverse * inverse
            cube = inverse_sq * inverse
            fifth = (cube * inverse_sq) * radial
            load = 0 if step == 0 else None
            high, low = split2(cube)
            pltpu.matmul_acc_lhs(plain_acc[step], high, load_staged_rhs=load)
            pltpu.matmul_acc_lhs(plain_acc[step], low)
            high, low = split2(fifth)
            pltpu.matmul_acc_lhs(cross_acc[step], high, load_staged_rhs=load)
            pltpu.matmul_acc_lhs(cross_acc[step], low)

    def close_chunk(offsets, first, plain_acc, cross_acc):
        half = tiles // 2
        for side, offset in enumerate(offsets):
            sums = [
                (pltpu.matmul_pop(plain_acc[t]) + pltpu.matmul_pop(cross_acc[t]))[:, :128]
                for t in range(side * half, (side + 1) * half)
            ]
            rows = jnp.transpose(jnp.concatenate(sums, axis=0))
            z, devices = devices_of(offset)
            state = sink_ref[devices[0]]
            for device in devices[1:]:
                state = state + sink_ref[device]
            pos = state[0:3]
            vel = state[3:6]
            whole = rows[18:19] + rows[19:20] + rows[20:21]
            cross = rows[21:22] + rows[22:23] + rows[23:24]
            new_acc = (rows[0:3] + rows[3:6] + rows[6:9]) - pos * whole
            new_jerk = (rows[9:12] + rows[12:15] + rows[15:18]) - vel * whole + pos * cross
            result = jnp.concatenate([new_acc, new_jerk, jnp.zeros((2, group), F32)], axis=0)
            part_ref[z] = result
            if first and side == 0:
                sum_ref[cut] = result
                devices = devices[1:]
            for device in devices:
                part_copy(z, cut, device).start()

    def compute(*accumulators):
        plain_acc = accumulators[:tiles]
        cross_acc = accumulators[tiles:]

        open_chunk((0, 1), True)

        def near_block(k, _):
            block = nth_block(k)

            @pl.when(k > 0)
            def _():
                star_copy(block, block).wait_recv()
                star_weights(block)

            pairs(block, plain_acc, cross_acc)
            return 0

        lax.fori_loop(0, teams, near_block, 0)
        close_chunk((0, 1), True, plain_acc, cross_acc)

        def one_chunk(g, _):
            offsets = (zs // 2 + 1 - g, zs // 2 + g)
            open_chunk(offsets, False)

            def next_block(k, _):
                pairs(k, plain_acc, cross_acc)
                return 0

            lax.fori_loop(0, teams, next_block, 0)
            close_chunk(offsets, False, plain_acc, cross_acc)
            return 0

        lax.fori_loop(1, zs // 2, one_chunk, 0)

    pl.run_scoped(
        compute,
        *[pltpu.ACC(0)((tile, 256), F32) for _ in range(tiles)],
        *[pltpu.ACC(1)((tile, 256), F32) for _ in range(tiles)],
    )

    def take_part(k, total):
        block = lax.rem(cut + k, cuts)
        part_copy(0, block, block).wait_recv()
        return total + sum_ref[block]

    total = lax.fori_loop(1, cuts, take_part, sum_ref[cut])
    total = jnp.where(lane_x == my_x, total, 0.0)
    rows = total[:, :slots]
    for x in range(1, xs):
        rows = rows + total[:, x * slots : (x + 1) * slots]
    own_rows = own_ref[...]
    is_live = lax.broadcasted_iota(jnp.int32, (1, slots), 1) < count_ref[...]
    out_ref[...] = correct(own_rows[0:6], own_rows[6:9], own_rows[9:12], rows, is_live)

    def end_star(k, _):
        star_copy(team, lax.rem(team + k, teams)).wait_send()
        return 0

    def end_sink(k, _):
        device = lax.rem(cut + k, cuts)
        sink_copy(cut, device).wait_send()
        part_copy(0, cut, device).wait_send()
        return 0

    lax.fori_loop(1, teams, end_star, 0)
    lax.fori_loop(1, cuts, end_sink, 0)


def solution(mesh):
    teams = mesh.shape["team"]
    cuts = mesh.shape["cuts"]
    xs = 4
    cores = 2

    def local(position, velocity, accel_old, jerk_old, star_mass, active_index, active_count):
        stars = position.shape[1]
        slots = active_index.shape[0]
        group = xs * slots
        vmem = pl.BlockSpec(memory_space=pltpu.VMEM)
        dma = pltpu.SemaphoreType.DMA
        return pl.pallas_call(
            functools.partial(step_kernel, teams, cuts, xs, slots, stars, cores),
            out_shape=jax.ShapeDtypeStruct((12, slots), F32),
            in_specs=[vmem] * 7,
            out_specs=vmem,
            scratch_shapes=[
                pltpu.VMEM((16, slots), F32),
                pltpu.VMEM((teams, 8, stars), F32),
                pltpu.VMEM((cuts, 8, group), F32),
                pltpu.VMEM((cuts // xs, 8, group), F32),
                pltpu.VMEM((cuts, 8, group), F32),
                pltpu.VMEM((teams, 256, stars), BF16),
                pltpu.VMEM((teams, 256, stars), BF16),
                pltpu.VMEM((6, 2 * group, 128), F32),
                dma((teams,)), dma((teams,)), dma((cuts,)), dma((cuts,)), dma((cuts,)), dma((cuts,)),
            ],
            compiler_params=pltpu.CompilerParams(collective_id=0, has_side_effects=True),
            name="hermite_step",
        )(
            position, velocity, accel_old, jerk_old,
            star_mass.reshape(1, stars), active_index.reshape(1, slots), active_count.reshape(1, 1),
        )

    column = P(None, ("team", "cuts"))
    line = P(("team", "cuts"))
    return jax.shard_map(
        local, mesh=mesh, in_specs=(column, column, column, column, line, line, line),
        out_specs=column, check_vma=False,
    )
```

time: 57.2 us -> 51.5 us (0.900)
  Pallas kernels: 55.1 us -> 49.3 us
    pallas_call x1, Pallas kernels: 55.1 us -> 49.3 us  [local(): pl.pallas_call(functools.partial(step_kernel, teams, cuts, xs, slots, sta...]
where the time goes in v2:
time: 51.5 us; the launch traced here: 51.3 us
  Pallas kernels  49.3 us (96%)
  local copies, waits for them, and re-layouts  1.3 us (3%)
  between operations  0.66 us (1%)
    pallas_call x1, Pallas kernels, local(): pl.pallas_call(functools.partial(step_kernel, teams, cuts, xs, slots, sta...  49.3 us
    unnamed x1, local copies, waits for them, and re-layouts  1.3 us

profile of v2, /device:TPU:1, one launch (start us, length us, event | category | flops | bytes accessed | tf_op | source)
XLA Modules:
  0.0 51.3 jit_solution(4145470061364186873)
XLA Ops:
  0.7 49.3 %hermite_step.1 = f32[12,32]{1,0:T(8,128)} custom-call(f32[3,256]{1,0:T(4,128)} %pos_ref.1, f32[3,256]{1,0:T(4,128)} %vel_ref.1, f32[3,256]{1,0:T(4,128)} %acc_ref.1, f32[3,256]{1,0:T(4,128)} %jerk_ref.1, f32[1,256]{1,0:T(1,128)} %bitcast.4, s32[1,32]{1,0:T(1,128)} %bitcast.5, s32[1,1]{1,0:T(1,128)} %bitcast.3.count_ref), custom_call_target="tpu_custom_call" | custom-call | tf_op jit(solution)/shard_map/hermite_step/pallas_call | solution.py:329
  50.0 1.3 %copy.10 = f32[12,32]{1,0:T(8,128)} copy(f32[12,32]{1,0:T(8,128)} %hermite_step.1) | data formatting | bytes 3072

commit v3 on v2

v3 whole, which is shorter than its diff:
```python
import functools

import jax
import jax.numpy as jnp
from jax import lax
from jax.experimental import pallas as pl
from jax.experimental.pallas import tpu as pltpu
from jax.sharding import PartitionSpec as P

STEP_DT = 0.5
SOFTENING = 0.0004
MESH = pl.DeviceIdType.MESH
F32 = jnp.float32
BF16 = jnp.bfloat16


def split2(value):
    high = value.astype(BF16)
    return high, (value - high.astype(F32)).astype(BF16)


def split3(value):
    high = value.astype(BF16)
    rest = value - high.astype(F32)
    middle = rest.astype(BF16)
    return high, middle, (rest - middle.astype(F32)).astype(BF16)


def stack_pieces(rows, height):
    filled = sum(row.shape[0] for row in rows)
    rows = [row.astype(F32) for row in rows]
    rows = rows + [jnp.zeros((height - filled, rows[0].shape[1]), F32)]
    return jnp.concatenate(rows, axis=0).astype(BF16)


def predict(position, velocity, accel_old, jerk_old):
    pred_pos = position + STEP_DT * (
        velocity + STEP_DT * (accel_old * 0.5 + STEP_DT * (jerk_old * (1.0 / 6.0)))
    )
    pred_vel = velocity + STEP_DT * (accel_old + STEP_DT * (jerk_old * 0.5))
    return (pred_pos, pred_vel)


def correct(sink_state, old_acc, old_jerk, new_rows, is_live):
    pred_pos = sink_state[:3]
    pred_vel = sink_state[3:6]
    new_acc = new_rows[:3]
    new_jerk = new_rows[3:6]
    change = old_acc - new_acc
    second = -6.0 * change - STEP_DT * (4.0 * old_jerk + 2.0 * new_jerk)
    third = 12.0 * change + 6.0 * STEP_DT * (old_jerk + new_jerk)
    new_pos = pred_pos + STEP_DT * STEP_DT * (second * (1.0 / 24.0) + third * (1.0 / 120.0))
    new_vel = pred_vel + STEP_DT * (second * (1.0 / 6.0) + third * (1.0 / 24.0))
    stacked = jnp.concatenate([new_pos, new_vel, new_acc, new_jerk], axis=0)
    return jnp.where(is_live, stacked, 0.0)


def near_first(ys, zs):
    spans = [range(-((n - 1) // 2), n // 2 + 1) for n in (ys, zs)]
    return sorted(
        ((dy, dz) for dy in spans[0] for dz in spans[1]),
        key=lambda offset: (abs(offset[0]) + abs(offset[1]), abs(offset[0])),
    )


def looked_up(table, base, index):
    per_word = 1
    while base ** (per_word + 1) < 2**31:
        per_word += 1
    word_index = index // per_word
    place = lax.rem(index, per_word)
    word = jnp.int32(0)
    for n in range(-(-len(table) // per_word)):
        digits = table[n * per_word : (n + 1) * per_word]
        value = sum(digit * base**r for r, digit in enumerate(digits))
        word = jnp.where(word_index == n, jnp.int32(value), word)
    result = jnp.int32(0)
    for r in range(per_word):
        result = jnp.where(place == r, lax.rem(word // base**r, base), result)
    return result


def step_kernel(
    teams, cuts, xs, slots, stars, cores,
    pos_ref, vel_ref, acc_ref, jerk_ref, mass_ref, index_ref, count_ref, out_ref,
    own_ref, star_ref, sink_ref, part_ref, sum_ref, plain_ref, cross_ref, wide_ref,
    star_send, star_recv, sink_send, sink_recv, part_send, part_recv,
):
    team = lax.axis_index("team")
    cut = lax.axis_index("cuts")
    zs = cuts // xs
    ys = teams // cores
    my_z = cut // xs
    my_x = lax.rem(cut, xs)
    my_y = team // cores
    my_core = lax.rem(team, cores)
    group = xs * slots
    peers = cores * xs
    blocks = ys * zs
    tile = 16
    half_tiles = group // tile
    tiles = cores * half_tiles
    me = my_core * xs + my_x
    order = near_first(ys, zs)
    low_y, high_y = min(o[0] for o in order), max(o[0] for o in order)
    low_z, high_z = min(o[1] for o in order), max(o[1] for o in order)
    table = [(dy - low_y) * zs + (dz - low_z) for dy, dz in order]

    def peer_id(k):
        peer = lax.rem(me + k, peers)
        return (my_y * cores + peer // xs, my_z * xs + lax.rem(peer, xs))

    def side_id(dy, dz):
        y = lax.rem(my_y + dy + ys, ys)
        z = lax.rem(my_z + dz + zs, zs)
        return (y * cores + my_core, z * xs + my_x)

    sides = ((-1, 0), (1, 0), (0, -1), (0, 1))
    barrier = pltpu.get_barrier_semaphore()
    for dy, dz in sides:
        pl.semaphore_signal(barrier, inc=1, device_id=side_id(dy, dz), device_id_type=MESH)
    for k in range(1, peers):
        pl.semaphore_signal(barrier, inc=1, device_id=peer_id(k), device_id_type=MESH)

    acc_old = acc_ref[...]
    jerk_old = jerk_ref[...]
    pred_pos, pred_vel = predict(pos_ref[...], vel_ref[...], acc_old, jerk_old)
    weight = mass_ref[...] * (1.0 / (stars * teams * cuts))
    home = my_y * zs + my_z
    star_ref[home] = jnp.concatenate(
        [pred_pos, pred_vel, weight, jnp.zeros((1, stars), F32)], axis=0
    )
    index = jnp.concatenate(
        [index_ref[...], jnp.full((1, 256 - slots), -1, jnp.int32)], axis=1
    )
    picked = (
        lax.broadcasted_iota(jnp.int32, (stars, 256), 0) == index
    ).astype(F32).astype(BF16)
    source = jnp.concatenate([pred_pos, pred_vel, acc_old, jerk_old, jnp.zeros((4, stars), F32)], 0)

    def pick(pick_acc):
        pltpu.matmul_push_rhs(picked, staging_register=0, mxu_index=0)
        for n, piece in enumerate(split3(source)):
            pltpu.matmul_acc_lhs(pick_acc, piece, load_staged_rhs=0 if n == 0 else None)
        own_ref[...] = pltpu.matmul_pop(pick_acc)[:, :slots]

    pl.run_scoped(pick, pltpu.ACC(0)((16, 256), F32))
    own = own_ref[...]
    lane_x = lax.broadcasted_iota(jnp.int32, (8, group), 1) // slots
    state = jnp.concatenate([own[0:6], jnp.zeros((2, slots), F32)], axis=0)
    sink_ref[me] = jnp.where(lane_x == my_x, jnp.concatenate([state] * xs, axis=1), 0.0)

    def star_weights(block, buffer):
        state = star_ref[block]
        mass = state[6:7]
        mass_pos = mass * state[0:3]
        mass_vel = mass * state[3:6]
        empty3 = jnp.zeros((3, stars), F32)
        empty9 = jnp.zeros((9, stars), F32)
        plain_ref[buffer, :32, :] = stack_pieces(
            [*split3(mass_pos), *split3(mass_vel), *split3(mass), empty3], 32
        )
        cross_ref[buffer, :32, :] = stack_pieces(
            [empty9, *split3(-3.0 * mass_pos), empty3, *split3(3.0 * mass)], 32
        )

    plain_ref[...] = jnp.zeros_like(plain_ref)
    cross_ref[...] = jnp.zeros_like(cross_ref)
    star_weights(home, 0)

    pl.semaphore_wait(barrier, len(sides) + peers - 1)

    def sink_copy(k):
        return pltpu.make_async_remote_copy(
            src_ref=sink_ref.at[me], dst_ref=sink_ref.at[me],
            send_sem=sink_send, recv_sem=sink_recv,
            device_id=peer_id(k), device_id_type=MESH,
        )

    def part_copy(k):
        return pltpu.make_async_remote_copy(
            src_ref=part_ref.at[lax.rem(me + k, peers) // xs], dst_ref=sum_ref.at[me],
            send_sem=part_send, recv_sem=part_recv,
            device_id=peer_id(k), device_id_type=MESH,
        )

    def star_copy(block, side):
        return pltpu.make_async_remote_copy(
            src_ref=star_ref.at[block], dst_ref=star_ref.at[block],
            send_sem=star_send.at[side], recv_sem=star_recv.at[block],
            device_id=side_id(*sides[side]), device_id_type=MESH,
        )

    def all_but_me(ref, send_sem, recv_sem):
        return pltpu.make_async_remote_copy(
            src_ref=ref.at[pl.ds(0, peers - 1)], dst_ref=ref.at[pl.ds(0, peers - 1)],
            send_sem=send_sem, recv_sem=recv_sem,
            device_id=peer_id(1), device_id_type=MESH,
        )

    def place(k):
        code = looked_up(table, ys * zs, k)
        dy = code // zs + low_y
        dz = lax.rem(code, zs) + low_z
        y = lax.rem(my_y + dy + ys, ys)
        z = lax.rem(my_z + dz + zs, zs)
        return dy, dz, y * zs + z

    def relay(k):
        dy, dz, block = place(k)
        star_copy(block, 0).wait_recv()

        @pl.when((dz == 0) & (dy > 0) & (dy < high_y))
        def _():
            star_copy(block, 0).start()

        @pl.when((dz == 0) & (dy < 0) & (dy > low_y))
        def _():
            star_copy(block, 1).start()

        @pl.when((dz >= 0) & (dz < high_z))
        def _():
            star_copy(block, 2).start()

        @pl.when((dz <= 0) & (dz > low_z))
        def _():
            star_copy(block, 3).start()

    for k in range(1, peers):
        sink_copy(k).start()
    for side in range(4):
        star_copy(home, side).start()
    early = 5

    def relay_early(k, _):
        relay(k)
        return 0

    lax.fori_loop(1, early, relay_early, 0)
    all_but_me(sink_ref, sink_send, sink_recv).wait_recv()

    def core_state(core):
        state = sink_ref[core * xs]
        for x in range(1, xs):
            state = state + sink_ref[core * xs + x]
        return state

    for core in range(cores):
        columns = jnp.transpose(core_state(core))
        for c in range(6):
            wide_ref[c, core * group : (core + 1) * group, :] = jnp.broadcast_to(
                columns[:, c : c + 1], (group, 128)
            )

    def compute(*accumulators):
        plain_acc = accumulators[:tiles]
        cross_acc = accumulators[tiles:]

        def one_block(k, _):
            buffer = lax.rem(k, 2)
            pltpu.matmul_push_rhs(
                plain_ref[buffer], staging_register=0, mxu_index=0, transpose=True
            )
            pltpu.matmul_push_rhs(
                cross_ref[buffer], staging_register=0, mxu_index=1, transpose=True
            )

            @pl.when((k + 2 >= early) & (k + 2 < blocks))
            def _():
                relay(k + 2)

            _, _, block = place(k)
            state = star_ref[block]
            _, _, following = place(jnp.minimum(k + 1, blocks - 1))
            star_weights(following, 1 - buffer)
            for step in range(tiles):
                rows = slice(step * tile, (step + 1) * tile)
                sinks = [wide_ref[c, rows, :] for c in range(6)]
                sinks = [jnp.concatenate([value] * (stars // 128), axis=1) for value in sinks]
                sep = [state[c : c + 1] - sinks[c] for c in range(3)]
                rel = [state[3 + c : 4 + c] - sinks[3 + c] for c in range(3)]
                radius_sq = sep[0] * sep[0] + (sep[1] * sep[1] + (sep[2] * sep[2] + SOFTENING))
                radial = sep[0] * rel[0] + sep[1] * rel[1] + sep[2] * rel[2]
                inverse = lax.rsqrt(radius_sq)
                inverse_sq = inverse * inverse
                cube = inverse_sq * inverse
                fifth = (cube * inverse_sq) * radial
                load = 0 if step == 0 else None
                high, low = split2(cube)
                pltpu.matmul_acc_lhs(plain_acc[step], high, load_staged_rhs=load)
                pltpu.matmul_acc_lhs(plain_acc[step], low)
                high, low = split2(fifth)
                pltpu.matmul_acc_lhs(cross_acc[step], high, load_staged_rhs=load)
                pltpu.matmul_acc_lhs(cross_acc[step], low)
            return 0

        lax.fori_loop(0, blocks, one_block, 0)
        for core in range(cores):
            sums = [
                (pltpu.matmul_pop(plain_acc[t]) + pltpu.matmul_pop(cross_acc[t]))[:, :128]
                for t in range(core * half_tiles, (core + 1) * half_tiles)
            ]
            rows = jnp.transpose(jnp.concatenate(sums, axis=0))
            state = core_state(core)
            pos = state[0:3]
            vel = state[3:6]
            whole = rows[18:19] + rows[19:20] + rows[20:21]
            cross = rows[21:22] + rows[22:23] + rows[23:24]
            new_acc = (rows[0:3] + rows[3:6] + rows[6:9]) - pos * whole
            new_jerk = (rows[9:12] + rows[12:15] + rows[15:18]) - vel * whole + pos * cross
            part_ref[core] = jnp.concatenate(
                [new_acc, new_jerk, jnp.zeros((2, group), F32)], axis=0
            )

    pl.run_scoped(
        compute,
        *[pltpu.ACC(0)((tile, 256), F32) for _ in range(tiles)],
        *[pltpu.ACC(1)((tile, 256), F32) for _ in range(tiles)],
    )
    for k in range(1, peers):
        part_copy(k).start()
    sum_ref[me] = part_ref[my_core]
    all_but_me(sink_ref, sink_send, sink_recv).wait_send()
    counts = (high_y, -low_y, ys * high_z, -ys * low_z)
    for side in range(4):
        pltpu.make_async_remote_copy(
            src_ref=star_ref.at[pl.ds(0, counts[side])], dst_ref=star_ref.at[pl.ds(0, counts[side])],
            send_sem=star_send.at[side], recv_sem=star_recv.at[0],
            device_id=side_id(*sides[side]), device_id_type=MESH,
        ).wait_send()
    all_but_me(sum_ref, part_send, part_recv).wait_recv()

    total = sum_ref[0]
    for k in range(1, peers):
        total = total + sum_ref[k]
    total = jnp.where(lane_x == my_x, total, 0.0)
    rows = total[:, :slots]
    for x in range(1, xs):
        rows = rows + total[:, x * slots : (x + 1) * slots]
    own_rows = own_ref[...]
    is_live = lax.broadcasted_iota(jnp.int32, (1, slots), 1) < count_ref[...]
    out_ref[...] = correct(own_rows[0:6], own_rows[6:9], own_rows[9:12], rows, is_live)
    all_but_me(sum_ref, part_send, part_recv).wait_send()


def solution(mesh):
    teams = mesh.shape["team"]
    cuts = mesh.shape["cuts"]
    xs = 4
    cores = 2
    blocks = teams * cuts // (xs * cores)

    def local(position, velocity, accel_old, jerk_old, star_mass, active_index, active_count):
        stars = position.shape[1]
        slots = active_index.shape[0]
        group = xs * slots
        vmem = pl.BlockSpec(memory_space=pltpu.VMEM)
        dma = pltpu.SemaphoreType.DMA
        return pl.pallas_call(
            functools.partial(step_kernel, teams, cuts, xs, slots, stars, cores),
            out_shape=jax.ShapeDtypeStruct((12, slots), F32),
            in_specs=[vmem] * 7,
            out_specs=vmem,
            scratch_shapes=[
                pltpu.VMEM((16, slots), F32),
                pltpu.VMEM((blocks, 8, stars), F32),
                pltpu.VMEM((xs * cores, 8, group), F32),
                pltpu.VMEM((cores, 8, group), F32),
                pltpu.VMEM((xs * cores, 8, group), F32),
                pltpu.VMEM((2, 256, stars), BF16),
                pltpu.VMEM((2, 256, stars), BF16),
                pltpu.VMEM((6, cores * group, 128), F32),
                dma((4,)), dma((blocks,)), dma, dma, dma, dma,
            ],
            compiler_params=pltpu.CompilerParams(collective_id=0, has_side_effects=True),
            name="hermite_step",
        )(
            position, velocity, accel_old, jerk_old,
            star_mass.reshape(1, stars), active_index.reshape(1, slots), active_count.reshape(1, 1),
        )

    column = P(None, ("team", "cuts"))
    line = P(("team", "cuts"))
    return jax.shard_map(
        local, mesh=mesh, in_specs=(column, column, column, column, line, line, line),
        out_specs=column, check_vma=False,
    )
```

time: 51.5 us -> 57.3 us (1.11)
  Pallas kernels: 49.3 us -> 55.2 us
    pallas_call x1, Pallas kernels: 49.3 us -> 55.2 us  [local(): pl.pallas_call(functools.partial(step_kernel, teams, cuts, xs, slots, sta...]
where the time goes in v3:
time: 57.3 us; the launch traced here: 57.1 us
  Pallas kernels  55.2 us (96%)
  local copies, waits for them, and re-layouts  1.3 us (2%)
  between operations  0.66 us (1%)
    pallas_call x1, Pallas kernels, local(): pl.pallas_call(functools.partial(step_kernel, teams, cuts, xs, slots, sta...  55.2 us
    unnamed x1, local copies, waits for them, and re-layouts  1.3 us

profile of v3, /device:TPU:1, one launch (start us, length us, event | category | flops | bytes accessed | tf_op | source)
XLA Modules:
  0.0 57.1 jit_solution(4465671755445484345)
XLA Ops:
  0.7 55.2 %hermite_step.1 = f32[12,32]{1,0:T(8,128)} custom-call(f32[3,256]{1,0:T(4,128)} %pos_ref.1, f32[3,256]{1,0:T(4,128)} %vel_ref.1, f32[3,256]{1,0:T(4,128)} %acc_ref.1, f32[3,256]{1,0:T(4,128)} %jerk_ref.1, f32[1,256]{1,0:T(1,128)} %bitcast.4, s32[1,32]{1,0:T(1,128)} %bitcast.5, s32[1,1]{1,0:T(1,128)} %bitcast.3.count_ref), custom_call_target="tpu_custom_call" | custom-call | tf_op jit(solution)/shard_map/hermite_step/pallas_call | solution.py:359
  55.8 1.3 %copy.10 = f32[12,32]{1,0:T(8,128)} copy(f32[12,32]{1,0:T(8,128)} %hermite_step.1) | data formatting | bytes 3072

commit v4 on v3

--- a/solution.py
+++ b/solution.py
@@ -55,78 +55,53 @@
     return jnp.where(is_live, stacked, 0.0)
 
 
-def near_first(ys, zs):
-    spans = [range(-((n - 1) // 2), n // 2 + 1) for n in (ys, zs)]
-    return sorted(
-        ((dy, dz) for dy in spans[0] for dz in spans[1]),
-        key=lambda offset: (abs(offset[0]) + abs(offset[1]), abs(offset[0])),
-    )
-
-
-def looked_up(table, base, index):
-    per_word = 1
-    while base ** (per_word + 1) < 2**31:
-        per_word += 1
-    word_index = index // per_word
-    place = lax.rem(index, per_word)
-    word = jnp.int32(0)
-    for n in range(-(-len(table) // per_word)):
-        digits = table[n * per_word : (n + 1) * per_word]
-        value = sum(digit * base**r for r, digit in enumerate(digits))
-        word = jnp.where(word_index == n, jnp.int32(value), word)
-    result = jnp.int32(0)
-    for r in range(per_word):
-        result = jnp.where(place == r, lax.rem(word // base**r, base), result)
-    return result
-
-
 def step_kernel(
     teams, cuts, xs, slots, stars, cores,
     pos_ref, vel_ref, acc_ref, jerk_ref, mass_ref, index_ref, count_ref, out_ref,
     own_ref, star_ref, sink_ref, part_ref, sum_ref, plain_ref, cross_ref, wide_ref,
-    star_send, star_recv, sink_send, sink_recv, part_send, part_recv,
+    row_recv, half_recv, side_send, sink_send, sink_recv, part_send, part_recv,
 ):
     team = lax.axis_index("team")
     cut = lax.axis_index("cuts")
     zs = cuts // xs
     ys = teams // cores
-    my_z = cut // xs
-    my_x = lax.rem(cut, xs)
-    my_y = team // cores
-    my_core = lax.rem(team, cores)
+    my_y = team >> 1
+    my_core = team & 1
+    my_z = cut >> 2
+    my_x = cut & 3
     group = xs * slots
     peers = cores * xs
-    blocks = ys * zs
     tile = 16
     half_tiles = group // tile
     tiles = cores * half_tiles
     me = my_core * xs + my_x
-    order = near_first(ys, zs)
-    low_y, high_y = min(o[0] for o in order), max(o[0] for o in order)
-    low_z, high_z = min(o[1] for o in order), max(o[1] for o in order)
-    table = [(dy - low_y) * zs + (dz - low_z) for dy, dz in order]
-
-    def peer_id(k):
-        peer = lax.rem(me + k, peers)
-        return (my_y * cores + peer // xs, my_z * xs + lax.rem(peer, xs))
+    half = ys // 2
+    units = 2 * (zs - 1)
+    paired = units - 2
+
+    peer_steps = [(dc, dx) for dc in range(cores) for dx in range(xs)][1:]
+
+    def peer_id(step):
+        dc, dx = step
+        return (my_y * cores + ((my_core + dc) & 1), my_z * xs + ((my_x + dx) & 3))
 
     def side_id(dy, dz):
-        y = lax.rem(my_y + dy + ys, ys)
-        z = lax.rem(my_z + dz + zs, zs)
+        y = (my_y + dy) & (ys - 1)
+        z = (my_z + dz) & (zs - 1)
         return (y * cores + my_core, z * xs + my_x)
 
     sides = ((-1, 0), (1, 0), (0, -1), (0, 1))
     barrier = pltpu.get_barrier_semaphore()
     for dy, dz in sides:
         pl.semaphore_signal(barrier, inc=1, device_id=side_id(dy, dz), device_id_type=MESH)
-    for k in range(1, peers):
-        pl.semaphore_signal(barrier, inc=1, device_id=peer_id(k), device_id_type=MESH)
+    for step in peer_steps:
+        pl.semaphore_signal(barrier, inc=1, device_id=peer_id(step), device_id_type=MESH)
 
     acc_old = acc_ref[...]
     jerk_old = jerk_ref[...]
     pred_pos, pred_vel = predict(pos_ref[...], vel_ref[...], acc_old, jerk_old)
     weight = mass_ref[...] * (1.0 / (stars * teams * cuts))
-    home = my_y * zs + my_z
+    home = my_z * ys + my_y
     star_ref[home] = jnp.concatenate(
         [pred_pos, pred_vel, weight, jnp.zeros((1, stars), F32)], axis=0
     )
@@ -168,76 +143,98 @@
     cross_ref[...] = jnp.zeros_like(cross_ref)
     star_weights(home, 0)
 
-    pl.semaphore_wait(barrier, len(sides) + peers - 1)
-
-    def sink_copy(k):
+    pl.semaphore_wait(barrier, len(sides) + len(peer_steps))
+
+    def sink_copy(step):
         return pltpu.make_async_remote_copy(
             src_ref=sink_ref.at[me], dst_ref=sink_ref.at[me],
             send_sem=sink_send, recv_sem=sink_recv,
-            device_id=peer_id(k), device_id_type=MESH,
-        )
-
-    def part_copy(k):
-        return pltpu.make_async_remote_copy(
-            src_ref=part_ref.at[lax.rem(me + k, peers) // xs], dst_ref=sum_ref.at[me],
+            device_id=peer_id(step), device_id_type=MESH,
+        )
+
+    def part_copy(step):
+        return pltpu.make_async_remote_copy(
+            src_ref=part_ref.at[(my_core + step[0]) & 1], dst_ref=sum_ref.at[me],
             send_sem=part_send, recv_sem=part_recv,
-            device_id=peer_id(k), device_id_type=MESH,
-        )
-
-    def star_copy(block, side):
+            device_id=peer_id(step), device_id_type=MESH,
+        )
+
+    def row_copy(block, side, number):
         return pltpu.make_async_remote_copy(
             src_ref=star_ref.at[block], dst_ref=star_ref.at[block],
-            send_sem=star_send.at[side], recv_sem=star_recv.at[block],
+            send_sem=side_send.at[side], recv_sem=row_recv.at[number],
             device_id=side_id(*sides[side]), device_id_type=MESH,
         )
 
-    def all_but_me(ref, send_sem, recv_sem):
-        return pltpu.make_async_remote_copy(
-            src_ref=ref.at[pl.ds(0, peers - 1)], dst_ref=ref.at[pl.ds(0, peers - 1)],
+    def half_copy(block, side, unit, device):
+        return pltpu.make_async_remote_copy(
+            src_ref=star_ref.at[block], dst_ref=star_ref.at[block],
+            send_sem=side_send.at[side], recv_sem=half_recv.at[unit],
+            device_id=device, device_id_type=MESH,
+        )
+
+    def many(ref, count, send_sem, recv_sem):
+        return pltpu.make_async_remote_copy(
+            src_ref=ref.at[pl.ds(0, count)], dst_ref=ref.at[pl.ds(0, count)],
             send_sem=send_sem, recv_sem=recv_sem,
-            device_id=peer_id(1), device_id_type=MESH,
-        )
-
-    def place(k):
-        code = looked_up(table, ys * zs, k)
-        dy = code // zs + low_y
-        dz = lax.rem(code, zs) + low_z
-        y = lax.rem(my_y + dy + ys, ys)
-        z = lax.rem(my_z + dz + zs, zs)
-        return dy, dz, y * zs + z
-
-    def relay(k):
-        dy, dz, block = place(k)
-        star_copy(block, 0).wait_recv()
-
-        @pl.when((dz == 0) & (dy > 0) & (dy < high_y))
-        def _():
-            star_copy(block, 0).start()
-
-        @pl.when((dz == 0) & (dy < 0) & (dy > low_y))
-        def _():
-            star_copy(block, 1).start()
-
-        @pl.when((dz >= 0) & (dz < high_z))
-        def _():
-            star_copy(block, 2).start()
-
-        @pl.when((dz <= 0) & (dz > low_z))
-        def _():
-            star_copy(block, 3).start()
-
-    for k in range(1, peers):
-        sink_copy(k).start()
-    for side in range(4):
-        star_copy(home, side).start()
-    early = 5
-
-    def relay_early(k, _):
-        relay(k)
-        return 0
-
-    lax.fori_loop(1, early, relay_early, 0)
-    all_but_me(sink_ref, sink_send, sink_recv).wait_recv()
+            device_id=side_id(0, 1), device_id_type=MESH,
+        )
+
+    row = [(n + 1) // 2 * (1 if n & 1 else -1) for n in range(ys)]
+    high_y, low_y = max(row), min(row)
+    high_z, low_z = zs // 2, -((zs - 1) // 2)
+
+    def row_block(n):
+        return my_z * ys + ((my_y + row[n]) & (ys - 1))
+
+    def pass_on(n):
+        block = row_block(n)
+        dy = row[n]
+        if 0 <= dy < high_y:
+            row_copy(block, 0, row.index(dy + 1)).start()
+        if low_y < dy <= 0:
+            row_copy(block, 1, row.index(dy - 1)).start()
+        part = n // half
+        half_copy(block, 2, 2 * part, side_id(*sides[2])).start()
+        half_copy(block, 3, 2 * part + 1, side_id(*sides[3])).start()
+
+    def take_row(n):
+        row_copy(row_block(n), 0, n).wait_recv()
+        pass_on(n)
+
+    def unit_place(unit):
+        last = unit >= paired
+        distance = (unit >> 2) + 1
+        back = jnp.where(last, 0, unit & 1)
+        part = jnp.where(last, unit & 1, (unit >> 1) & 1)
+        dz = jnp.where(back == 1, -distance, distance)
+        return distance, back, part, (my_z + dz) & (zs - 1)
+
+    def unit_block(part, z, n):
+        number = part * half + n
+        dy = ((number + 1) >> 1) * (2 * (number & 1) - 1)
+        return z * ys + ((my_y + dy) & (ys - 1))
+
+    def take_unit(unit):
+        many(star_ref, half, side_send.at[0], half_recv.at[unit]).wait_recv()
+        distance, back, part, z = unit_place(unit)
+        following = jnp.where(unit < paired - 4, unit + 4, paired + part)
+        for side in (2, 3):
+            reach = high_z if side == 2 else -low_z
+
+            @pl.when((back == side - 2) & (distance < reach))
+            def _():
+                for n in range(half):
+                    half_copy(
+                        unit_block(part, z, n), side, following, side_id(*sides[side])
+                    ).start()
+
+    for step in peer_steps:
+        sink_copy(step).start()
+    pass_on(0)
+    take_row(1)
+    take_row(2)
+    many(sink_ref, peers - 1, sink_send, sink_recv).wait_recv()
 
     def core_state(core):
         state = sink_ref[core * xs]
@@ -256,22 +253,14 @@
         plain_acc = accumulators[:tiles]
         cross_acc = accumulators[tiles:]
 
-        def one_block(k, _):
-            buffer = lax.rem(k, 2)
+        def pairs(block, buffer, following):
             pltpu.matmul_push_rhs(
                 plain_ref[buffer], staging_register=0, mxu_index=0, transpose=True
             )
             pltpu.matmul_push_rhs(
                 cross_ref[buffer], staging_register=0, mxu_index=1, transpose=True
             )
-
-            @pl.when((k + 2 >= early) & (k + 2 < blocks))
-            def _():
-                relay(k + 2)
-
-            _, _, block = place(k)
             state = star_ref[block]
-            _, _, following = place(jnp.minimum(k + 1, blocks - 1))
             star_weights(following, 1 - buffer)
             for step in range(tiles):
                 rows = slice(step * tile, (step + 1) * tile)
@@ -292,9 +281,37 @@
                 high, low = split2(fifth)
                 pltpu.matmul_acc_lhs(cross_acc[step], high, load_staged_rhs=load)
                 pltpu.matmul_acc_lhs(cross_acc[step], low)
+
+        for n in range(ys):
+            if n & 1 and n + 2 < ys:
+                take_row(n + 2)
+                if n + 3 < ys:
+                    take_row(n + 3)
+            if n + 1 == ys:
+                take_unit(0)
+                _, _, part, z = unit_place(0)
+                following = unit_block(part, z, 0)
+            else:
+                following = row_block(n + 1)
+            pairs(row_block(n), n & 1, following)
+
+        def one_unit(unit, _):
+            @pl.when(unit + 1 < units)
+            def _():
+                take_unit(unit + 1)
+
+            _, _, part, z = unit_place(unit)
+            _, _, next_part, next_z = unit_place(jnp.minimum(unit + 1, units - 1))
+            for n in range(half):
+                block = unit_block(part, z, n)
+                if n + 1 < half:
+                    following = unit_block(part, z, n + 1)
+                else:
+                    following = unit_block(next_part, next_z, 0)
+                pairs(block, n & 1, following)
             return 0
 
-        lax.fori_loop(0, blocks, one_block, 0)
+        lax.fori_loop(0, units, one_unit, 0)
         for core in range(cores):
             sums = [
                 (pltpu.matmul_pop(plain_acc[t]) + pltpu.matmul_pop(cross_acc[t]))[:, :128]
@@ -317,18 +334,13 @@
         *[pltpu.ACC(0)((tile, 256), F32) for _ in range(tiles)],
         *[pltpu.ACC(1)((tile, 256), F32) for _ in range(tiles)],
     )
-    for k in range(1, peers):
-        part_copy(k).start()
+    for step in peer_steps:
+        part_copy(step).start()
     sum_ref[me] = part_ref[my_core]
-    all_but_me(sink_ref, sink_send, sink_recv).wait_send()
-    counts = (high_y, -low_y, ys * high_z, -ys * low_z)
-    for side in range(4):
-        pltpu.make_async_remote_copy(
-            src_ref=star_ref.at[pl.ds(0, counts[side])], dst_ref=star_ref.at[pl.ds(0, counts[side])],
-            send_sem=star_send.at[side], recv_sem=star_recv.at[0],
-            device_id=side_id(*sides[side]), device_id_type=MESH,
-        ).wait_send()
-    all_but_me(sum_ref, part_send, part_recv).wait_recv()
+    many(sink_ref, peers - 1, sink_send, sink_recv).wait_send()
+    for side, count in enumerate((high_y, -low_y, ys * high_z, -ys * low_z)):
+        many(star_ref, count, side_send.at[side], row_recv.at[0]).wait_send()
+    many(sum_ref, peers - 1, part_send, part_recv).wait_recv()
 
     total = sum_ref[0]
     for k in range(1, peers):
@@ -340,7 +352,7 @@
     own_rows = own_ref[...]
     is_live = lax.broadcasted_iota(jnp.int32, (1, slots), 1) < count_ref[...]
     out_ref[...] = correct(own_rows[0:6], own_rows[6:9], own_rows[9:12], rows, is_live)
-    all_but_me(sum_ref, part_send, part_recv).wait_send()
+    many(sum_ref, peers - 1, part_send, part_recv).wait_send()
 
 
 def solution(mesh):
@@ -370,7 +382,7 @@
                 pltpu.VMEM((2, 256, stars), BF16),
                 pltpu.VMEM((2, 256, stars), BF16),
                 pltpu.VMEM((6, cores * group, 128), F32),
-                dma((4,)), dma((blocks,)), dma, dma, dma, dma,
+                dma((teams // cores,)), dma((2 * (cuts // xs - 1),)), dma((4,)), dma, dma, dma, dma,
             ],
             compiler_params=pltpu.CompilerParams(collective_id=0, has_side_effects=True),
             name="hermite_step",

time: 57.3 us -> 50.4 us (0.88)
  Pallas kernels: 55.2 us -> 48.3 us
    pallas_call x1, Pallas kernels: 55.2 us -> 48.3 us  [local(): pl.pallas_call(functools.partial(step_kernel, teams, cuts, xs, slots, sta...]
where the time goes in v4:
time: 50.4 us; the launch traced here: 50.2 us
  Pallas kernels  48.3 us (96%)
  local copies, waits for them, and re-layouts  1.3 us (3%)
  between operations  0.66 us (1%)
    pallas_call x1, Pallas kernels, local(): pl.pallas_call(functools.partial(step_kernel, teams, cuts, xs, slots, sta...  48.3 us
    unnamed x1, local copies, waits for them, and re-layouts  1.3 us

profile of v4, /device:TPU:1, one launch (start us, length us, event | category | flops | bytes accessed | tf_op | source)
XLA Modules:
  0.0 50.2 jit_solution(6995408335765966755)
XLA Ops:
  0.7 48.3 %hermite_step.1 = f32[12,32]{1,0:T(8,128)} custom-call(f32[3,256]{1,0:T(4,128)} %pos_ref.1, f32[3,256]{1,0:T(4,128)} %vel_ref.1, f32[3,256]{1,0:T(4,128)} %acc_ref.1, f32[3,256]{1,0:T(4,128)} %jerk_ref.1, f32[1,256]{1,0:T(1,128)} %bitcast.4, s32[1,32]{1,0:T(1,128)} %bitcast.5, s32[1,1]{1,0:T(1,128)} %bitcast.3.count_ref), custom_call_target="tpu_custom_call" | custom-call | tf_op jit(solution)/shard_map/hermite_step/pallas_call | solution.py:371
  48.9 1.3 %copy.10 = f32[12,32]{1,0:T(8,128)} copy(f32[12,32]{1,0:T(8,128)} %hermite_step.1) | data formatting | bytes 3072

commit v5 on v4

--- a/solution.py
+++ b/solution.py
@@ -59,24 +59,25 @@
     teams, cuts, xs, slots, stars, cores,
     pos_ref, vel_ref, acc_ref, jerk_ref, mass_ref, index_ref, count_ref, out_ref,
     own_ref, star_ref, sink_ref, part_ref, sum_ref, plain_ref, cross_ref, wide_ref,
-    row_recv, half_recv, side_send, sink_send, sink_recv, part_send, part_recv,
+    row_recv, half_recv, row_send, half_send, sink_send, sink_recv, part_send, part_recv,
 ):
     team = lax.axis_index("team")
     cut = lax.axis_index("cuts")
-    zs = cuts // xs
-    ys = teams // cores
+    side = teams // cores
     my_y = team >> 1
     my_core = team & 1
     my_z = cut >> 2
     my_x = cut & 3
+    first = jnp.where(my_core == 0, my_y, my_z)
+    second = jnp.where(my_core == 0, my_z, my_y)
     group = xs * slots
     peers = cores * xs
     tile = 16
     half_tiles = group // tile
     tiles = cores * half_tiles
     me = my_core * xs + my_x
-    half = ys // 2
-    units = 2 * (zs - 1)
+    half = side // 2
+    units = 2 * (side - 1)
     paired = units - 2
 
     peer_steps = [(dc, dx) for dc in range(cores) for dx in range(xs)][1:]
@@ -85,15 +86,18 @@
         dc, dx = step
         return (my_y * cores + ((my_core + dc) & 1), my_z * xs + ((my_x + dx) & 3))
 
-    def side_id(dy, dz):
-        y = (my_y + dy) & (ys - 1)
-        z = (my_z + dz) & (zs - 1)
+    def ring_id(d_first, d_second):
+        u = (first + d_first) & (side - 1)
+        w = (second + d_second) & (side - 1)
+        y = jnp.where(my_core == 0, u, w)
+        z = jnp.where(my_core == 0, w, u)
         return (y * cores + my_core, z * xs + my_x)
 
-    sides = ((-1, 0), (1, 0), (0, -1), (0, 1))
+    row = [(n + 1) // 2 * (1 if n & 1 else -1) for n in range(side)]
     barrier = pltpu.get_barrier_semaphore()
-    for dy, dz in sides:
-        pl.semaphore_signal(barrier, inc=1, device_id=side_id(dy, dz), device_id_type=MESH)
+    for offset in row[1:]:
+        pl.semaphore_signal(barrier, inc=1, device_id=ring_id(offset, 0), device_id_type=MESH)
+        pl.semaphore_signal(barrier, inc=1, device_id=ring_id(0, offset), device_id_type=MESH)
     for step in peer_steps:
         pl.semaphore_signal(barrier, inc=1, device_id=peer_id(step), device_id_type=MESH)
 
@@ -101,7 +105,7 @@
     jerk_old = jerk_ref[...]
     pred_pos, pred_vel = predict(pos_ref[...], vel_ref[...], acc_old, jerk_old)
     weight = mass_ref[...] * (1.0 / (stars * teams * cuts))
-    home = my_z * ys + my_y
+    home = second * side + first
     star_ref[home] = jnp.concatenate(
         [pred_pos, pred_vel, weight, jnp.zeros((1, stars), F32)], axis=0
     )
@@ -143,7 +147,7 @@
     cross_ref[...] = jnp.zeros_like(cross_ref)
     star_weights(home, 0)
 
-    pl.semaphore_wait(barrier, len(sides) + len(peer_steps))
+    pl.semaphore_wait(barrier, 2 * (side - 1) + len(peer_steps))
 
     def sink_copy(step):
         return pltpu.make_async_remote_copy(
@@ -159,47 +163,43 @@
             device_id=peer_id(step), device_id_type=MESH,
         )
 
-    def row_copy(block, side, number):
+    def row_copy(block, number, offset):
         return pltpu.make_async_remote_copy(
             src_ref=star_ref.at[block], dst_ref=star_ref.at[block],
-            send_sem=side_send.at[side], recv_sem=row_recv.at[number],
-            device_id=side_id(*sides[side]), device_id_type=MESH,
-        )
-
-    def half_copy(block, side, unit, device):
+            send_sem=row_send, recv_sem=row_recv.at[number],
+            device_id=ring_id(offset, 0), device_id_type=MESH,
+        )
+
+    def half_copy(block, unit, offset):
         return pltpu.make_async_remote_copy(
             src_ref=star_ref.at[block], dst_ref=star_ref.at[block],
-            send_sem=side_send.at[side], recv_sem=half_recv.at[unit],
-            device_id=device, device_id_type=MESH,
+            send_sem=half_send, recv_sem=half_recv.at[unit],
+            device_id=ring_id(0, offset), device_id_type=MESH,
         )
 
     def many(ref, count, send_sem, recv_sem):
         return pltpu.make_async_remote_copy(
             src_ref=ref.at[pl.ds(0, count)], dst_ref=ref.at[pl.ds(0, count)],
             send_sem=send_sem, recv_sem=recv_sem,
-            device_id=side_id(0, 1), device_id_type=MESH,
-        )
-
-    row = [(n + 1) // 2 * (1 if n & 1 else -1) for n in range(ys)]
-    high_y, low_y = max(row), min(row)
-    high_z, low_z = zs // 2, -((zs - 1) // 2)
+            device_id=peer_id((0, 1)), device_id_type=MESH,
+        )
 
     def row_block(n):
-        return my_z * ys + ((my_y + row[n]) & (ys - 1))
+        return second * side + ((first + row[n]) & (side - 1))
+
+    def unit_of(offset, part):
+        if offset == side // 2:
+            return paired + part
+        return 4 * (abs(offset) - 1) + 2 * part + (1 if offset < 0 else 0)
 
     def pass_on(n):
         block = row_block(n)
-        dy = row[n]
-        if 0 <= dy < high_y:
-            row_copy(block, 0, row.index(dy + 1)).start()
-        if low_y < dy <= 0:
-            row_copy(block, 1, row.index(dy - 1)).start()
-        part = n // half
-        half_copy(block, 2, 2 * part, side_id(*sides[2])).start()
-        half_copy(block, 3, 2 * part + 1, side_id(*sides[3])).start()
+        for offset in row[1:]:
+            seen = -offset if offset != side // 2 else offset
+            half_copy(block, unit_of(seen, n // half), offset).start()
 
     def take_row(n):
-        row_copy(row_block(n), 0, n).wait_recv()
+        row_copy(row_block(n), n, row[1]).wait_recv()
         pass_on(n)
 
     def unit_place(unit):
@@ -207,33 +207,25 @@
         distance = (unit >> 2) + 1
         back = jnp.where(last, 0, unit & 1)
         part = jnp.where(last, unit & 1, (unit >> 1) & 1)
-        dz = jnp.where(back == 1, -distance, distance)
-        return distance, back, part, (my_z + dz) & (zs - 1)
-
-    def unit_block(part, z, n):
+        offset = jnp.where(back == 1, -distance, distance)
+        return part, (second + offset) & (side - 1)
+
+    def unit_block(part, w, n):
         number = part * half + n
-        dy = ((number + 1) >> 1) * (2 * (number & 1) - 1)
-        return z * ys + ((my_y + dy) & (ys - 1))
+        offset = ((number + 1) >> 1) * (2 * (number & 1) - 1)
+        return w * side + ((first + offset) & (side - 1))
 
     def take_unit(unit):
-        many(star_ref, half, side_send.at[0], half_recv.at[unit]).wait_recv()
-        distance, back, part, z = unit_place(unit)
-        following = jnp.where(unit < paired - 4, unit + 4, paired + part)
-        for side in (2, 3):
-            reach = high_z if side == 2 else -low_z
-
-            @pl.when((back == side - 2) & (distance < reach))
-            def _():
-                for n in range(half):
-                    half_copy(
-                        unit_block(part, z, n), side, following, side_id(*sides[side])
-                    ).start()
+        many(star_ref, half, half_send, half_recv.at[unit]).wait_recv()
 
     for step in peer_steps:
         sink_copy(step).start()
+    for n in range(1, side):
+        seen = -row[n] if row[n] != side // 2 else row[n]
+        row_copy(home, row.index(seen), row[n]).start()
     pass_on(0)
-    take_row(1)
-    take_row(2)
+    for n in range(1, 5):
+        take_row(n)
     many(sink_ref, peers - 1, sink_send, sink_recv).wait_recv()
 
     def core_state(core):
@@ -282,15 +274,16 @@
                 pltpu.matmul_acc_lhs(cross_acc[step], high, load_staged_rhs=load)
                 pltpu.matmul_acc_lhs(cross_acc[step], low)
 
-        for n in range(ys):
-            if n & 1 and n + 2 < ys:
-                take_row(n + 2)
-                if n + 3 < ys:
-                    take_row(n + 3)
-            if n + 1 == ys:
+        for n in range(side):
+            if n == 1:
+                take_row(5)
+                take_row(6)
+            if n == 3:
+                take_row(7)
+            if n + 1 == side:
                 take_unit(0)
-                _, _, part, z = unit_place(0)
-                following = unit_block(part, z, 0)
+                part, w = unit_place(0)
+                following = unit_block(part, w, 0)
             else:
                 following = row_block(n + 1)
             pairs(row_block(n), n & 1, following)
@@ -300,14 +293,14 @@
             def _():
                 take_unit(unit + 1)
 
-            _, _, part, z = unit_place(unit)
-            _, _, next_part, next_z = unit_place(jnp.minimum(unit + 1, units - 1))
+            part, w = unit_place(unit)
+            next_part, next_w = unit_place(jnp.minimum(unit + 1, units - 1))
             for n in range(half):
-                block = unit_block(part, z, n)
+                block = unit_block(part, w, n)
                 if n + 1 < half:
-                    following = unit_block(part, z, n + 1)
+                    following = unit_block(part, w, n + 1)
                 else:
-                    following = unit_block(next_part, next_z, 0)
+                    following = unit_block(next_part, next_w, 0)
                 pairs(block, n & 1, following)
             return 0
 
@@ -338,8 +331,8 @@
         part_copy(step).start()
     sum_ref[me] = part_ref[my_core]
     many(sink_ref, peers - 1, sink_send, sink_recv).wait_send()
-    for side, count in enumerate((high_y, -low_y, ys * high_z, -ys * low_z)):
-        many(star_ref, count, side_send.at[side], row_recv.at[0]).wait_send()
+    many(star_ref, side - 1, row_send, row_recv.at[0]).wait_send()
+    many(star_ref, side * (side - 1), half_send, half_recv.at[0]).wait_send()
     many(sum_ref, peers - 1, part_send, part_recv).wait_recv()
 
     total = sum_ref[0]
@@ -382,7 +375,7 @@
                 pltpu.VMEM((2, 256, stars), BF16),
                 pltpu.VMEM((2, 256, stars), BF16),
                 pltpu.VMEM((6, cores * group, 128), F32),
-                dma((teams // cores,)), dma((2 * (cuts // xs - 1),)), dma((4,)), dma, dma, dma, dma,
+                dma((teams // cores,)), dma((2 * (cuts // xs - 1),)), dma, dma, dma, dma, dma, dma,
             ],
             compiler_params=pltpu.CompilerParams(collective_id=0, has_side_effects=True),
             name="hermite_step",

time: 50.4 us -> 46.6 us (0.925)
  Pallas kernels: 48.3 us -> 44.4 us
    pallas_call x1, Pallas kernels: 48.3 us -> 44.4 us  [local(): pl.pallas_call(functools.partial(step_kernel, teams, cuts, xs, slots, sta...]
where the time goes in v5:
time: 46.6 us; the launch traced here: 46.4 us
  Pallas kernels  44.4 us (95%)
  local copies, waits for them, and re-layouts  1.3 us (3%)
  between operations  0.66 us (1%)
    pallas_call x1, Pallas kernels, local(): pl.pallas_call(functools.partial(step_kernel, teams, cuts, xs, slots, sta...  44.4 us
    unnamed x1, local copies, waits for them, and re-layouts  1.3 us

profile of v5, /device:TPU:1, one launch (start us, length us, event | category | flops | bytes accessed | tf_op | source)
XLA Modules:
  0.0 46.4 jit_solution(17242799445076890591)
XLA Ops:
  0.7 44.4 %hermite_step.1 = f32[12,32]{1,0:T(8,128)} custom-call(f32[3,256]{1,0:T(4,128)} %pos_ref.1, f32[3,256]{1,0:T(4,128)} %vel_ref.1, f32[3,256]{1,0:T(4,128)} %acc_ref.1, f32[3,256]{1,0:T(4,128)} %jerk_ref.1, f32[1,256]{1,0:T(1,128)} %bitcast.4, s32[1,32]{1,0:T(1,128)} %bitcast.5, s32[1,1]{1,0:T(1,128)} %bitcast.3.count_ref), custom_call_target="tpu_custom_call" | custom-call | tf_op jit(solution)/shard_map/hermite_step/pallas_call | solution.py:364
  45.1 1.3 %copy.10 = f32[12,32]{1,0:T(8,128)} copy(f32[12,32]{1,0:T(8,128)} %hermite_step.1) | data formatting | bytes 3072

commit v6 on v5

--- a/solution.py
+++ b/solution.py
@@ -57,7 +57,8 @@
 
 def step_kernel(
     teams, cuts, xs, slots, stars, cores,
-    pos_ref, vel_ref, acc_ref, jerk_ref, mass_ref, index_ref, count_ref, out_ref,
+    pos_hbm, vel_hbm, acc_hbm, jerk_hbm, mass_hbm, index_hbm, count_hbm, out_ref,
+    pos_ref, vel_ref, acc_ref, jerk_ref, mass_ref, index_ref, count_ref, load_sem,
     own_ref, star_ref, sink_ref, part_ref, sum_ref, plain_ref, cross_ref, wide_ref,
     row_recv, half_recv, row_send, half_send, sink_send, sink_recv, part_send, part_recv,
 ):
@@ -101,6 +102,20 @@
     for step in peer_steps:
         pl.semaphore_signal(barrier, inc=1, device_id=peer_id(step), device_id_type=MESH)
 
+    loads = [
+        pltpu.make_async_copy(source, target, load_sem.at[n])
+        for n, (source, target) in enumerate((
+            (pos_hbm, pos_ref), (vel_hbm, vel_ref), (acc_hbm, acc_ref), (jerk_hbm, jerk_ref),
+            (mass_hbm, mass_ref), (index_hbm, index_ref), (count_hbm, count_ref),
+        ))
+    ]
+    for load in loads:
+        load.start()
+    plain_ref[...] = jnp.zeros_like(plain_ref)
+    cross_ref[...] = jnp.zeros_like(cross_ref)
+    for load in loads:
+        load.wait()
+
     acc_old = acc_ref[...]
     jerk_old = jerk_ref[...]
     pred_pos, pred_vel = predict(pos_ref[...], vel_ref[...], acc_old, jerk_old)
@@ -143,8 +158,6 @@
             [empty9, *split3(-3.0 * mass_pos), empty3, *split3(3.0 * mass)], 32
         )
 
-    plain_ref[...] = jnp.zeros_like(plain_ref)
-    cross_ref[...] = jnp.zeros_like(cross_ref)
     star_weights(home, 0)
 
     pl.semaphore_wait(barrier, 2 * (side - 1) + len(peer_steps))
@@ -224,8 +237,6 @@
         seen = -row[n] if row[n] != side // 2 else row[n]
         row_copy(home, row.index(seen), row[n]).start()
     pass_on(0)
-    for n in range(1, 5):
-        take_row(n)
     many(sink_ref, peers - 1, sink_send, sink_recv).wait_recv()
 
     def core_state(core):
@@ -253,7 +264,8 @@
                 cross_ref[buffer], staging_register=0, mxu_index=1, transpose=True
             )
             state = star_ref[block]
-            star_weights(following, 1 - buffer)
+            if following is not None:
+                star_weights(following, 1 - buffer)
             for step in range(tiles):
                 rows = slice(step * tile, (step + 1) * tile)
                 sinks = [wide_ref[c, rows, :] for c in range(6)]
@@ -274,19 +286,34 @@
                 pltpu.matmul_acc_lhs(cross_acc[step], high, load_staged_rhs=load)
                 pltpu.matmul_acc_lhs(cross_acc[step], low)
 
-        for n in range(side):
-            if n == 1:
-                take_row(5)
-                take_row(6)
-            if n == 3:
-                take_row(7)
-            if n + 1 == side:
-                take_unit(0)
-                part, w = unit_place(0)
-                following = unit_block(part, w, 0)
-            else:
-                following = row_block(n + 1)
-            pairs(row_block(n), n & 1, following)
+        def near_block(kind, number, n=0):
+            if kind == "row":
+                return row_block(number)
+            return unit_block(*unit_place(number), n)
+
+        near = [("row", n) for n in range(5)]
+        near += [("unit", unit, n) for unit in (0, 1) for n in range(half)]
+        near += [("row", n) for n in (5, 6, 7)]
+        near += [("unit", unit, n) for unit in (2, 3) for n in range(half)]
+        near += [("unit", 4, 0)]
+        takes = {
+            ("row", 1): [(take_row, 1), (take_row, 2)],
+            ("row", 2): [(take_row, 3), (take_row, 4)],
+            ("row", 4): [(take_unit, 0)],
+            ("unit", 0, 2): [(take_row, 5), (take_row, 6)],
+            ("unit", 0, 3): [(take_unit, 1)],
+            ("row", 6): [(take_row, 7)],
+            ("row", 7): [(take_unit, 2)],
+            ("unit", 2, 3): [(take_unit, 3)],
+            ("unit", 3, 3): [(take_unit, 4)],
+        }
+        for position, here in enumerate(near[:-1]):
+            for take, number in takes.get(here, ()):
+                take(number)
+            if position == 1:
+                star_weights(near_block(*here), 1)
+            following = None if position == 0 else near_block(*near[position + 1])
+            pairs(near_block(*here), position & 1, following)
 
         def one_unit(unit, _):
             @pl.when(unit + 1 < units)
@@ -304,7 +331,7 @@
                 pairs(block, n & 1, following)
             return 0
 
-        lax.fori_loop(0, units, one_unit, 0)
+        lax.fori_loop(4, units, one_unit, 0)
         for core in range(cores):
             sums = [
                 (pltpu.matmul_pop(plain_acc[t]) + pltpu.matmul_pop(cross_acc[t]))[:, :128]
@@ -364,9 +391,14 @@
         return pl.pallas_call(
             functools.partial(step_kernel, teams, cuts, xs, slots, stars, cores),
             out_shape=jax.ShapeDtypeStruct((12, slots), F32),
-            in_specs=[vmem] * 7,
+            in_specs=[pl.BlockSpec(memory_space=pl.ANY)] * 7,
             out_specs=vmem,
             scratch_shapes=[
+                *[pltpu.VMEM((3, stars), F32) for _ in range(4)],
+                pltpu.VMEM((1, stars), F32),
+                pltpu.VMEM((1, slots), jnp.int32),
+                pltpu.VMEM((1, 1), jnp.int32),
+                dma((7,)),
                 pltpu.VMEM((16, slots), F32),
                 pltpu.VMEM((blocks, 8, stars), F32),
                 pltpu.VMEM((xs * cores, 8, group), F32),

time: 46.6 us -> 47.5 us (1.019)
  Pallas kernels: 44.4 us -> 45.4 us
    pallas_call x1, Pallas kernels: 44.4 us -> 45.4 us  [local(): pl.pallas_call(functools.partial(step_kernel, teams, cuts, xs, slots, sta...]
where the time goes in v6:
time: 47.5 us; the launch traced here: 47.3 us
  Pallas kernels  45.4 us (96%)
  local copies, waits for them, and re-layouts  1.3 us (3%)
  between operations  0.66 us (1%)
    pallas_call x1, Pallas kernels, local(): pl.pallas_call(functools.partial(step_kernel, teams, cuts, xs, slots, sta...  45.4 us
    unnamed x1, local copies, waits for them, and re-layouts  1.3 us

profile of v6, /device:TPU:1, one launch (start us, length us, event | category | flops | bytes accessed | tf_op | source)
XLA Modules:
  0.0 47.3 jit_solution(16364620350235646442)
XLA Ops:
  0.7 45.4 %hermite_step.1 = f32[12,32]{1,0:T(8,128)} custom-call(f32[3,256]{1,0:T(4,128)} %pos_hbm.1, f32[3,256]{1,0:T(4,128)} %vel_hbm.1, f32[3,256]{1,0:T(4,128)} %acc_hbm.1, f32[3,256]{1,0:T(4,128)} %jerk_hbm.1, f32[1,256]{1,0:T(1,128)} %bitcast.4, s32[1,32]{1,0:T(1,128)} %bitcast.5, s32[1,1]{1,0:T(1,128)} %bitcast.3.count_hbm), custom_call_target="tpu_custom_call" | custom-call | tf_op jit(solution)/shard_map/hermite_step/pallas_call | solution.py:391
  46.0 1.3 %copy.10 = f32[12,32]{1,0:T(8,128)} copy(f32[12,32]{1,0:T(8,128)} %hermite_step.1) | data formatting | bytes 3072

commit v7 on v6

--- a/solution.py
+++ b/solution.py
@@ -264,8 +264,7 @@
                 cross_ref[buffer], staging_register=0, mxu_index=1, transpose=True
             )
             state = star_ref[block]
-            if following is not None:
-                star_weights(following, 1 - buffer)
+            star_weights(following, 1 - buffer)
             for step in range(tiles):
                 rows = slice(step * tile, (step + 1) * tile)
                 sinks = [wide_ref[c, rows, :] for c in range(6)]
@@ -291,29 +290,18 @@
                 return row_block(number)
             return unit_block(*unit_place(number), n)
 
-        near = [("row", n) for n in range(5)]
-        near += [("unit", unit, n) for unit in (0, 1) for n in range(half)]
-        near += [("row", n) for n in (5, 6, 7)]
-        near += [("unit", unit, n) for unit in (2, 3) for n in range(half)]
-        near += [("unit", 4, 0)]
+        near = [("row", n) for n in range(side)] + [("unit", 0, 0)]
         takes = {
-            ("row", 1): [(take_row, 1), (take_row, 2)],
-            ("row", 2): [(take_row, 3), (take_row, 4)],
-            ("row", 4): [(take_unit, 0)],
-            ("unit", 0, 2): [(take_row, 5), (take_row, 6)],
-            ("unit", 0, 3): [(take_unit, 1)],
-            ("row", 6): [(take_row, 7)],
-            ("row", 7): [(take_unit, 2)],
-            ("unit", 2, 3): [(take_unit, 3)],
-            ("unit", 3, 3): [(take_unit, 4)],
+            ("row", 0): [(take_row, 1), (take_row, 2)],
+            ("row", 1): [(take_row, 3), (take_row, 4)],
+            ("row", 3): [(take_row, 5), (take_row, 6)],
+            ("row", 5): [(take_row, 7)],
+            ("row", 7): [(take_unit, 0)],
         }
         for position, here in enumerate(near[:-1]):
             for take, number in takes.get(here, ()):
                 take(number)
-            if position == 1:
-                star_weights(near_block(*here), 1)
-            following = None if position == 0 else near_block(*near[position + 1])
-            pairs(near_block(*here), position & 1, following)
+            pairs(near_block(*here), position & 1, near_block(*near[position + 1]))
 
         def one_unit(unit, _):
             @pl.when(unit + 1 < units)
@@ -331,7 +319,7 @@
                 pairs(block, n & 1, following)
             return 0
 
-        lax.fori_loop(4, units, one_unit, 0)
+        lax.fori_loop(0, units, one_unit, 0)
         for core in range(cores):
             sums = [
                 (pltpu.matmul_pop(plain_acc[t]) + pltpu.matmul_pop(cross_acc[t]))[:, :128]

time: 47.5 us -> 46.7 us (0.983)
  Pallas kernels: 45.4 us -> 44.5 us
    pallas_call x1, Pallas kernels: 45.4 us -> 44.5 us  [local(): pl.pallas_call(functools.partial(step_kernel, teams, cuts, xs, slots, sta...]
where the time goes in v7:
time: 46.7 us; the launch traced here: 46.5 us
  Pallas kernels  44.5 us (95%)
  local copies, waits for them, and re-layouts  1.3 us (3%)
  between operations  0.66 us (1%)
    pallas_call x1, Pallas kernels, local(): pl.pallas_call(functools.partial(step_kernel, teams, cuts, xs, slots, sta...  44.5 us
    unnamed x1, local copies, waits for them, and re-layouts  1.3 us

profile of v7, /device:TPU:1, one launch (start us, length us, event | category | flops | bytes accessed | tf_op | source)
XLA Modules:
  0.0 46.5 jit_solution(13626723541857129917)
XLA Ops:
  0.7 44.5 %hermite_step.1 = f32[12,32]{1,0:T(8,128)} custom-call(f32[3,256]{1,0:T(4,128)} %pos_hbm.1, f32[3,256]{1,0:T(4,128)} %vel_hbm.1, f32[3,256]{1,0:T(4,128)} %acc_hbm.1, f32[3,256]{1,0:T(4,128)} %jerk_hbm.1, f32[1,256]{1,0:T(1,128)} %bitcast.4, s32[1,32]{1,0:T(1,128)} %bitcast.5, s32[1,1]{1,0:T(1,128)} %bitcast.3.count_hbm), custom_call_target="tpu_custom_call" | custom-call | tf_op jit(solution)/shard_map/hermite_step/pallas_call | solution.py:379
  45.2 1.3 %copy.10 = f32[12,32]{1,0:T(8,128)} copy(f32[12,32]{1,0:T(8,128)} %hermite_step.1) | data formatting | bytes 3072

commit v8 on v7

--- a/solution.py
+++ b/solution.py
@@ -264,7 +264,8 @@
                 cross_ref[buffer], staging_register=0, mxu_index=1, transpose=True
             )
             state = star_ref[block]
-            star_weights(following, 1 - buffer)
+            if following is not None:
+                star_weights(following, 1 - buffer)
             for step in range(tiles):
                 rows = slice(step * tile, (step + 1) * tile)
                 sinks = [wide_ref[c, rows, :] for c in range(6)]
@@ -293,9 +294,9 @@
         near = [("row", n) for n in range(side)] + [("unit", 0, 0)]
         takes = {
             ("row", 0): [(take_row, 1), (take_row, 2)],
-            ("row", 1): [(take_row, 3), (take_row, 4)],
-            ("row", 3): [(take_row, 5), (take_row, 6)],
-            ("row", 5): [(take_row, 7)],
+            ("row", 2): [(take_row, 3), (take_row, 4)],
+            ("row", 4): [(take_row, 5), (take_row, 6)],
+            ("row", 6): [(take_row, 7)],
             ("row", 7): [(take_unit, 0)],
         }
         for position, here in enumerate(near[:-1]):
@@ -303,23 +304,24 @@
                 take(number)
             pairs(near_block(*here), position & 1, near_block(*near[position + 1]))
 
-        def one_unit(unit, _):
-            @pl.when(unit + 1 < units)
-            def _():
-                take_unit(unit + 1)
-
+        def one_unit(unit, last=False):
             part, w = unit_place(unit)
-            next_part, next_w = unit_place(jnp.minimum(unit + 1, units - 1))
             for n in range(half):
-                block = unit_block(part, w, n)
                 if n + 1 < half:
                     following = unit_block(part, w, n + 1)
+                elif last:
+                    following = None
                 else:
-                    following = unit_block(next_part, next_w, 0)
-                pairs(block, n & 1, following)
+                    take_unit(unit + 1)
+                    following = unit_block(*unit_place(unit + 1), 0)
+                pairs(unit_block(part, w, n), n & 1, following)
+
+        def next_unit(unit, _):
+            one_unit(unit)
             return 0
 
-        lax.fori_loop(0, units, one_unit, 0)
+        lax.fori_loop(0, units - 1, next_unit, 0)
+        one_unit(jnp.int32(units - 1), last=True)
         for core in range(cores):
             sums = [
                 (pltpu.matmul_pop(plain_acc[t]) + pltpu.matmul_pop(cross_acc[t]))[:, :128]

time: 46.7 us -> 46.2 us (0.989)
  Pallas kernels: 44.5 us -> 44 us
    pallas_call x1, Pallas kernels: 44.5 us -> 44 us  [local(): pl.pallas_call(functools.partial(step_kernel, teams, cuts, xs, slots, sta...]
where the time goes in v8:
time: 46.2 us; the launch traced here: 46 us
  Pallas kernels  44 us (95%)
  local copies, waits for them, and re-layouts  1.3 us (3%)
  between operations  0.66 us (1%)
    pallas_call x1, Pallas kernels, local(): pl.pallas_call(functools.partial(step_kernel, teams, cuts, xs, slots, sta...  44 us
    unnamed x1, local copies, waits for them, and re-layouts  1.3 us

profile of v8, /device:TPU:1, one launch (start us, length us, event | category | flops | bytes accessed | tf_op | source)
XLA Modules:
  0.0 46.0 jit_solution(3866721317456863959)
XLA Ops:
  0.7 44.0 %hermite_step.1 = f32[12,32]{1,0:T(8,128)} custom-call(f32[3,256]{1,0:T(4,128)} %pos_hbm.1, f32[3,256]{1,0:T(4,128)} %vel_hbm.1, f32[3,256]{1,0:T(4,128)} %acc_hbm.1, f32[3,256]{1,0:T(4,128)} %jerk_hbm.1, f32[1,256]{1,0:T(1,128)} %bitcast.4, s32[1,32]{1,0:T(1,128)} %bitcast.5, s32[1,1]{1,0:T(1,128)} %bitcast.3.count_hbm), custom_call_target="tpu_custom_call" | custom-call | tf_op jit(solution)/shard_map/hermite_step/pallas_call | solution.py:381
  44.7 1.3 %copy.10 = f32[12,32]{1,0:T(8,128)} copy(f32[12,32]{1,0:T(8,128)} %hermite_step.1) | data formatting | bytes 3072

commit v9 on v8

--- a/solution.py
+++ b/solution.py
@@ -81,7 +81,7 @@
     units = 2 * (side - 1)
     paired = units - 2
 
-    peer_steps = [(dc, dx) for dc in range(cores) for dx in range(xs)][1:]
+    peer_steps = [(dc, dx) for dx in (2, 1, 3, 0) for dc in range(cores) if dc or dx]
 
     def peer_id(step):
         dc, dx = step
@@ -96,7 +96,7 @@
 
     row = [(n + 1) // 2 * (1 if n & 1 else -1) for n in range(side)]
     barrier = pltpu.get_barrier_semaphore()
-    for offset in row[1:]:
+    for offset in reversed(row[1:]):
         pl.semaphore_signal(barrier, inc=1, device_id=ring_id(offset, 0), device_id_type=MESH)
         pl.semaphore_signal(barrier, inc=1, device_id=ring_id(0, offset), device_id_type=MESH)
     for step in peer_steps:
@@ -347,9 +347,6 @@
     for step in peer_steps:
         part_copy(step).start()
     sum_ref[me] = part_ref[my_core]
-    many(sink_ref, peers - 1, sink_send, sink_recv).wait_send()
-    many(star_ref, side - 1, row_send, row_recv.at[0]).wait_send()
-    many(star_ref, side * (side - 1), half_send, half_recv.at[0]).wait_send()
     many(sum_ref, peers - 1, part_send, part_recv).wait_recv()
 
     total = sum_ref[0]
@@ -362,6 +359,9 @@
     own_rows = own_ref[...]
     is_live = lax.broadcasted_iota(jnp.int32, (1, slots), 1) < count_ref[...]
     out_ref[...] = correct(own_rows[0:6], own_rows[6:9], own_rows[9:12], rows, is_live)
+    many(sink_ref, peers - 1, sink_send, sink_recv).wait_send()
+    many(star_ref, side - 1, row_send, row_recv.at[0]).wait_send()
+    many(star_ref, side * (side - 1), half_send, half_recv.at[0]).wait_send()
     many(sum_ref, peers - 1, part_send, part_recv).wait_send()
 
 

time: 46.2 us -> 46 us (level)
  no operation moved by 1% of the time
where the time goes in v9:
time: 46 us; the launch traced here: 45.8 us
  Pallas kernels  43.8 us (95%)
  local copies, waits for them, and re-layouts  1.3 us (3%)
  between operations  0.66 us (1%)
    pallas_call x1, Pallas kernels, local(): pl.pallas_call(functools.partial(step_kernel, teams, cuts, xs, slots, sta...  43.8 us
    unnamed x1, local copies, waits for them, and re-layouts  1.3 us

profile of v9, /device:TPU:1, one launch (start us, length us, event | category | flops | bytes accessed | tf_op | source)
XLA Modules:
  0.0 45.8 jit_solution(15840507670239006225)
XLA Ops:
  0.7 43.8 %hermite_step.1 = f32[12,32]{1,0:T(8,128)} custom-call(f32[3,256]{1,0:T(4,128)} %pos_hbm.1, f32[3,256]{1,0:T(4,128)} %vel_hbm.1, f32[3,256]{1,0:T(4,128)} %acc_hbm.1, f32[3,256]{1,0:T(4,128)} %jerk_hbm.1, f32[1,256]{1,0:T(1,128)} %bitcast.4, s32[1,32]{1,0:T(1,128)} %bitcast.5, s32[1,1]{1,0:T(1,128)} %bitcast.3.count_hbm), custom_call_target="tpu_custom_call" | custom-call | tf_op jit(solution)/shard_map/hermite_step/pallas_call | solution.py:381
  44.5 1.3 %copy.10 = f32[12,32]{1,0:T(8,128)} copy(f32[12,32]{1,0:T(8,128)} %hermite_step.1) | data formatting | bytes 3072
